TPU v7x, 32 devices: a whole 2x2x4 slice. The times are simulated.
32 devices in a mesh: dp: 32 (over z, y, x, core).
Axes of the slice: x: 2, y: 2, z: 4, core: 2. Of those that a mesh axis runs over, the one named last changes fastest.
Arguments:
- tokens: float32 [64, 197, 384], P('dp'), may hold values from -6 to 6
- params: float32 [1774080], P('dp'), as said below
- moment1: float32 [1774080], P('dp'), may hold values from -0.0625 to 0.0625
- moment2: float32 [1774080], P('dp'), may hold values from 1e-06 to 1e-05
- cotangent: float32 [64, 197, 384], P('dp'), may hold values from -6 to 6
Outputs:
- result: float32 [64, 197, 384], P('dp')
- grad_tokens: float32 [64, 197, 384], P('dp')
- grad_params: float32 [1774080], P('dp')
- new_params: float32 [1774080], P('dp')
- new_moment1: float32 [1774080], P('dp')
- new_moment2: float32 [1774080], P('dp')
Inputs may be any that keep to these rules, and one draw needn't show every extreme that they name: `params`: finite floats.
All inputs are finite; a program needn't handle non-finite values.
Results may differ from a plain program's by a relative error of at most 0.0071.
The roundings to bfloat16 on the way count: a program that leaves them out, or rounds other values in their place, can miss the bound.
Values may be sent and summed in bfloat16 or wider, within the bound.
A program may use at most 128 MiB of HBM per device.

v0:
```python
import math

import jax
import jax.numpy as jnp
from jax import lax
from jax.sharding import PartitionSpec as P

D = 384
HEADS = 6
FF = 1536
SEQ = 197
MICRO = 2
STEP = 3


def product(spec, left, right):
    return jnp.einsum(spec, left, right, preferred_element_type=jnp.float32)


def token_sum(left, right):
    return lax.dot_general(
        left, right, (((0,), (0,)), ((), ())), preferred_element_type=jnp.float32
    )


def times_t(left, right):
    return lax.dot_general(
        left, right, (((1,), (1,)), ((), ())), preferred_element_type=jnp.float32
    )


def layer_norm(values):
    center = values - jnp.mean(values, axis=-1, keepdims=True)
    factor = lax.rsqrt(jnp.mean(center * center, axis=-1, keepdims=True) + 1e-06)
    return (center * factor, factor)


def norm_back(grad_hat, normed, factor):
    return factor * (
        grad_hat
        - jnp.mean(grad_hat, axis=-1, keepdims=True)
        - normed * jnp.mean(grad_hat * normed, axis=-1, keepdims=True)
    )


def unpack(flat):
    first = 3 * D * D
    second = first + D * D
    third = second + D * FF
    fourth = third + FF * D
    fifth = fourth + 8 * D
    return (
        flat[:first].reshape(D, 3 * D),
        flat[first:second].reshape(D, D),
        flat[second:third].reshape(D, FF),
        flat[third:fourth].reshape(FF, D),
        flat[fourth:fifth].astype(jnp.float32).reshape(8, D),
        flat[fifth:].astype(jnp.float32),
    )


def forward(tokens_mb, weights):
    w_qkv, w_out, w_up, w_down, vectors, up_bias = weights
    batch, length, width = tokens_mb.shape
    normed_in, scale_in = layer_norm(tokens_mb)
    attn_input = (normed_in * vectors[0] + vectors[1]).astype(jnp.bfloat16).reshape(-1, width)
    projected = jnp.dot(attn_input, w_qkv, preferred_element_type=jnp.float32)
    heads_shape = (batch, length, HEADS, width // HEADS)
    query_half = (projected[:, :width] + vectors[2]).astype(jnp.bfloat16).reshape(heads_shape)
    key_half = projected[:, width : 2 * width].astype(jnp.bfloat16).reshape(heads_shape)
    value_half = (projected[:, 2 * width :] + vectors[3]).astype(jnp.bfloat16).reshape(heads_shape)
    scores = product("bqhe,bkhe->bhqk", query_half, key_half) * (width // HEADS) ** (-0.5)
    top = jnp.max(scores, axis=-1, keepdims=True)
    raw_weights = jnp.exp(scores - top)
    total = jnp.sum(raw_weights, axis=-1, keepdims=True)
    log_total = top + jnp.log(total)
    probs = (raw_weights / total).astype(jnp.bfloat16)
    context = product("bhqk,bkhe->bqhe", probs, value_half).astype(jnp.bfloat16).reshape(-1, width)
    hidden_mid = tokens_mb + (
        jnp.dot(context, w_out, preferred_element_type=jnp.float32) + vectors[4]
    ).reshape(tokens_mb.shape)
    normed_mid, scale_mid = layer_norm(hidden_mid)
    mlp_input = (normed_mid * vectors[5] + vectors[6]).astype(jnp.bfloat16).reshape(-1, width)
    pre_act = jnp.dot(mlp_input, w_up, preferred_element_type=jnp.float32) + up_bias
    activated = jax.nn.gelu(pre_act, approximate=False).astype(jnp.bfloat16)
    result = hidden_mid + (
        jnp.dot(activated, w_down, preferred_element_type=jnp.float32) + vectors[7]
    ).reshape(tokens_mb.shape)
    saved = (
        normed_in,
        scale_in,
        attn_input,
        query_half,
        key_half,
        value_half,
        log_total,
        context,
        normed_mid,
        scale_mid,
        mlp_input,
        pre_act,
        activated,
    )
    return (result, saved)


def backward(saved, grad_result, weights):
    w_qkv, w_out, w_up, w_down, vectors, up_bias = weights
    (
        normed_in,
        scale_in,
        attn_input,
        query_half,
        key_half,
        value_half,
        log_total,
        context,
        normed_mid,
        scale_mid,
        mlp_input,
        pre_act,
        activated,
    ) = saved
    width = grad_result.shape[-1]
    grad_flat = grad_result.reshape(-1, width)
    grad_half = grad_flat.astype(jnp.bfloat16)
    grad_down = token_sum(activated, grad_half)
    grad_act = times_t(grad_half, w_down)
    slope = (
        0.5 * (1.0 + jax.scipy.special.erf(pre_act * 0.7071067811865476))
        + pre_act * jnp.exp(-0.5 * pre_act * pre_act) * 0.3989422804014327
    )
    grad_pre = grad_act * slope
    grad_pre_half = grad_pre.astype(jnp.bfloat16)
    grad_up = token_sum(mlp_input, grad_pre_half)
    grad_mlp_in = times_t(grad_pre_half, w_up)
    mid_flat = normed_mid.reshape(-1, width)
    grad_hidden = grad_result + norm_back(
        (grad_mlp_in * vectors[5]).reshape(grad_result.shape), normed_mid, scale_mid
    )
    hidden_flat = grad_hidden.reshape(-1, width)
    hidden_half = hidden_flat.astype(jnp.bfloat16)
    grad_wout = token_sum(context, hidden_half)
    grad_context = times_t(hidden_half, w_out).astype(jnp.bfloat16).reshape(query_half.shape)
    scale_factor = (width // HEADS) ** (-0.5)
    scores = product("bqhe,bkhe->bhqk", query_half, key_half) * scale_factor
    probs_full = jnp.exp(scores - log_total)
    probs_half = probs_full.astype(jnp.bfloat16)
    grad_value = product("bhqk,bqhe->bkhe", probs_half, grad_context)
    grad_probs = product("bqhe,bkhe->bhqk", grad_context, value_half)
    delta = jnp.sum(probs_full * grad_probs, axis=-1, keepdims=True)
    grad_scores = (probs_full * (grad_probs - delta) * scale_factor).astype(jnp.bfloat16)
    grad_query = product("bhqk,bkhe->bqhe", grad_scores, key_half).reshape(-1, width)
    grad_key = product("bhqk,bqhe->bkhe", grad_scores, query_half).reshape(-1, width)
    grad_value = grad_value.reshape(-1, width)
    proj_half = jnp.concatenate([grad_query, grad_key, grad_value], axis=1).astype(jnp.bfloat16)
    grad_wqkv = token_sum(attn_input, proj_half)
    grad_attn_in = times_t(proj_half, w_qkv)
    in_flat = normed_in.reshape(-1, width)
    grad_tokens = grad_hidden + norm_back(
        (grad_attn_in * vectors[0]).reshape(grad_result.shape), normed_in, scale_in
    )
    vector_grads = jnp.stack(
        [
            jnp.sum(grad_attn_in * in_flat, axis=0),
            jnp.sum(grad_attn_in, axis=0),
            jnp.sum(grad_query, axis=0),
            jnp.sum(grad_value, axis=0),
            jnp.sum(hidden_flat, axis=0),
            jnp.sum(grad_mlp_in * mid_flat, axis=0),
            jnp.sum(grad_mlp_in, axis=0),
            jnp.sum(grad_flat, axis=0),
        ]
    )
    flat = jnp.concatenate(
        [
            grad_wqkv.reshape(-1),
            grad_wout.reshape(-1),
            grad_up.reshape(-1),
            grad_down.reshape(-1),
            vector_grads.reshape(-1),
            jnp.sum(grad_pre, axis=0),
        ]
    )
    return (grad_tokens, flat)


def adamw(params, grads, first, second, position):
    first_end = 3 * D * D
    second_end = first_end + D * D
    third_end = second_end + D * FF
    fourth_end = third_end + FF * D
    rate = jnp.where(
        position < first_end,
        0.01,
        jnp.where(
            position < second_end,
            0.1,
            jnp.where(position < third_end, 0.01, jnp.where(position < fourth_end, 0.005, 0.1)),
        ),
    )
    first_new = 0.9 * first + 0.1 * grads
    second_new = 0.999 * second + 0.001 * grads * grads
    update = (
        first_new / (1.0 - 0.9**STEP) / (jnp.sqrt(second_new / (1.0 - 0.999**STEP)) + 1e-08)
        + 0.1 * params
    )
    return (params - rate * update, first_new, second_new)


def per_device(tokens, params, moment1, moment2, cotangent):
    shard_half = params.astype(jnp.bfloat16)
    blocks = tokens.reshape(MICRO, -1, SEQ, D)
    grad_blocks = cotangent.reshape(MICRO, -1, SEQ, D)
    results = []
    grads_in = []
    running = None
    shares = None
    for micro in range(MICRO):
        fwd_weights = unpack(lax.all_gather(shard_half, "dp", axis=0, tiled=True))
        result, saved = forward(blocks[micro], fwd_weights)
        bwd_weights = unpack(lax.all_gather(shard_half, "dp", axis=0, tiled=True))
        grad_in, flat = backward(saved, grad_blocks[micro], bwd_weights)
        results.append(result)
        grads_in.append(grad_in)
        running = flat if running is None else running + flat
    shares = lax.psum_scatter(running, "dp", scatter_dimension=0, tiled=True)
    count = tokens.shape[0] * tokens.shape[1] * lax.axis_size("dp")
    grad_params = shares * (1.0 / math.sqrt(count))
    length = params.shape[0]
    position = lax.axis_index("dp") * length + jnp.arange(length, dtype=jnp.int32)
    new_params, new_first, new_second = adamw(params, grad_params, moment1, moment2, position)
    result_all = jnp.concatenate(results, axis=0)
    grad_all = jnp.concatenate(grads_in, axis=0)
    return (result_all, grad_all, grad_params, new_params, new_first, new_second)


def solution(mesh):
    in_specs = (P("dp", None, None), P("dp"), P("dp"), P("dp"), P("dp", None, None))
    out_specs = (P("dp", None, None), P("dp", None, None), P("dp"), P("dp"), P("dp"), P("dp"))
    return jax.shard_map(
        per_device, mesh=mesh, in_specs=in_specs, out_specs=out_specs, check_vma=False
    )
```

profile of v0, /device:TPU:0, one launch (start us, length us, event | category | flops | bytes accessed | tf_op | source)
XLA Modules:
  0.0 458.9 jit_solution(16236229659665175842)
XLA Ops:
  7.2 1.6 convert_element_type.127
  9.1 2.2 dynamic-update-slice
  11.3 1.8 copy-done
  13.2 4.8 %slice_reduce_fusion = (f32[384]{0:T(512)S(1)}, f32[384]{0:T(512)S(1)}, f32[1,197,384]{2,0,1:T(1,128)}, f32[1,197,384]{2,0,1:T(1,128)}, f32[1,197,384]{2,0,1:T(1...) fusion(f32[2,197,384]{2,0,1:T(2,128)} %param.9, f32[2,197,384]{2,0,1:T(2,128)} %param.5), kind=kLoop, calls=%fused_computation.259 | loop fusion | flops 301430 | bytes 2425384 | tf_op jit(solution)/shard_map/reduce_sum | solution.py:172
  19.6 136.4 %all-reduce.5.cloned.1.call-done = bf16[1774080]{0:T(1024)(128)(2,1)} async-done(((bf16[1774080]{0:T(1024)(128)(2,1)}), bf16[1774080]{0:T(1024)(128)(2,1)}) %all-reduce.5.cloned.1.call-update) | async-done | bytes 3548176
  163.8 3.3 fusion.172
  167.1 3.5 slice.171
  171.8 3.1 slice.174
  180.6 3.8 fusion.17
  184.5 3.8 fusion.14
  188.3 1.4 fusion.187
  190.9 1.4 fusion.186
  194.0 1.6 fusion.170
  198.3 2.3 fusion.189
  200.7 2.3 fusion.173
  203.0 3.1 convolution_convert_fusion
  206.1 3.8 fusion.174
  209.9 1.3 log_add_fusion.1
  211.2 2.1 convolution_convert_fusion.5
  214.4 2.3 fusion.188
  216.7 1.6 fusion.175
  218.3 3.1 convolution_convert_fusion.1
  221.4 3.6 fusion.176
  225.0 2.2 fusion.125
  227.2 2.8 fusion.102
  230.7 1.9 fusion.108
  233.8 2.1 fusion.98
  235.8 1.8 fusion.110
  239.4 1.5 reshape.595
  240.9 1.3 constant_dynamic-update-slice_fusion.10
  242.2 1.9 reshape.596
  244.1 3.2 reshape.597
  247.4 2.0 fusion.135
  249.4 3.2 reshape.598
  252.9 1.5 reshape.602
  254.4 1.4 constant_dynamic-update-slice_fusion.11
  257.0 3.2 reshape.604
  260.2 2.1 fusion.132
  262.3 3.3 reshape.605
  266.8 3.4 constant_dynamic-update-slice_fusion.6
  270.1 1.6 constant_dynamic-update-slice_fusion.4
  273.9 1.6 constant_dynamic-update-slice_fusion.7
  275.4 1.7 constant_dynamic-update-slice_fusion.5
  278.8 5.4 %add.247 = f32[1774080]{0:T(1024)} add(f32[1774080]{0:T(1024)S(1)} %copy-done.1, f32[1774080]{0:T(1024)} %constant_dynamic-update-slice_fusion.1) | non-fusion elementwise | flops 1774080 | bytes 21288960 | tf_op jit(solution)/shard_map/add | solution.py:226
  284.3 1.2 copy-done.5
  285.5 1.6 fusion.46
  290.4 159.5 %all-reduce.7.cloned.1.call-done = f32[1774080]{0:T(1024)} async-done(((f32[1774080]{0:T(1024)}), f32[1774080]{0:T(1024)}) %all-reduce.7.cloned.1.call-update) | async-done | bytes 7096336
  449.9 2.1 multiply_subtract_fusion
  (277 shorter events, 36.1 us)
Async XLA Ops:
  7.2 148.8 %all-reduce.5.cloned.1.call-start = ((), (), s32[]{:S(2)}) async-start(), calls=%async_computation | async-start | bytes 7098368
  13.1 436.8 %all-reduce.7.cloned.1.call-start = ((), (), s32[]{:S(2)}) async-start(), calls=%async_computation.1 | async-start | bytes 14196736
  19.3 139.6 %copy-start.55 = (f32[197]{0:T(256)}, f32[197]{0:T(256)S(1)}, u32[]{:S(2)}) copy-start(f32[197]{0:T(256)S(1)} %broadcast_multiply_fusion.11) | copy-start | bytes 2368
  19.5 138.8 %copy-start.64 = (f32[197]{0:T(256)}, f32[197]{0:T(256)S(1)}, u32[]{:S(2)}) copy-start(f32[197]{0:T(256)S(1)} %add_rsqrt_fusion.1) | copy-start | bytes 2368
  19.6 139.3 %copy-start.66 = (f32[197]{0:T(256)}, f32[197]{0:T(256)S(1)}, u32[]{:S(2)}) copy-start(f32[197]{0:T(256)S(1)} %add_rsqrt_fusion.3) | copy-start | bytes 2368
  157.4 13.2 %copy-start.72 = (f32[384]{0:T(512)}, f32[384]{0:T(512)S(1)}, u32[]{:S(2)}) copy-start(f32[384]{0:T(512)S(1)} %get-tuple-element.73) | copy-start | bytes 4612
  163.1 7.5 %copy-start.44 = (bf16[6,64,197]{2,1,0:T(8,128)(2,1)}, bf16[6,64,197]{2,1,0:T(8,128)(2,1)S(1)}, u32[]{:S(2)}) copy-start(bf16[6,64,197]{2,1,0:T(8,128)(2,1)S(1)} %convolution_convert_fusion.2) | copy-start | bytes 453892
  163.8 6.8 %copy-start.10 = (bf16[384,384]{1,0:T(8,128)(2,1)}, bf16[384,384]{1,0:T(8,128)(2,1)S(1)}, u32[]{:S(2)}) copy-start(bf16[384,384]{1,0:T(8,128)(2,1)S(1)} %slice.166) | copy-start | bytes 884740
  171.0 3.9 copy-start.57
  171.2 3.7 copy-start.48
  171.8 3.9 copy-start.47
  179.4 14.6 %copy-start.60 = (f32[197]{0:T(256)}, f32[197]{0:T(256)S(1)}, u32[]{:S(2)}) copy-start(f32[197]{0:T(256)S(1)} %broadcast_multiply_fusion.10) | copy-start | bytes 2368
  180.2 13.7 %copy-start.70 = (f32[197]{0:T(256)}, f32[197]{0:T(256)S(1)}, u32[]{:S(2)}) copy-start(f32[197]{0:T(256)S(1)} %add_rsqrt_fusion.2) | copy-start | bytes 2368
  184.5 3.8 copy-start.4
  184.5 3.8 copy-start.25
  203.0 3.1 copy-start.37
  211.2 5.5 %copy-start.3 = (f32[6,197,197]{1,2,0:T(8,128)S(1)}, f32[6,197,197]{1,2,0:T(8,128)}, u32[]{:S(2)}) copy-start(f32[6,197,197]{1,2,0:T(8,128)} %copy-done.2) | copy-start | bytes 2794252
  211.2 5.5 %copy-start.63 = (f32[6,197]{1,0:T(8,128)S(1)}, f32[6,197]{1,0:T(8,128)}, u32[]{:S(2)}) copy-start(f32[6,197]{1,0:T(8,128)} %log_add_fusion.1) | copy-start | bytes 14188
  218.3 3.1 copy-start.41
  221.4 5.8 %copy-start.61 = (f32[197]{0:T(256)S(1)}, f32[197]{0:T(256)}, u32[]{:S(2)}) copy-start(f32[197]{0:T(256)} %copy-done.60) | copy-start | bytes 2368
  221.4 5.8 %copy-start.71 = (f32[197]{0:T(256)S(1)}, f32[197]{0:T(256)}, u32[]{:S(2)}) copy-start(f32[197]{0:T(256)} %copy-done.70) | copy-start | bytes 2368
  230.7 7.7 %copy-start.29 = (f32[197,384]{1,0:T(8,128)}, f32[197,384]{1,0:T(8,128)S(1)}, u32[]{:S(2)}) copy-start(f32[197,384]{1,0:T(8,128)S(1)} %fusion.109) | copy-start | bytes 907780
  230.7 3.0 copy-start.21
  230.7 3.0 copy-start.59
  230.7 3.0 copy-start.69
  244.1 3.2 copy-start.17
  244.1 3.2 copy-start.28
  249.4 3.3 copy-start.90
  249.4 3.4 copy-start.78
  249.4 3.4 copy-start.84
  249.4 3.4 copy-start.83
  249.4 3.5 copy-start.82
  249.4 3.5 copy-start.88
  256.9 3.2 copy-start.19
  257.0 3.2 copy-start.26
  262.3 3.4 copy-start.89
  262.3 3.4 copy-start.77
  262.3 3.5 copy-start.81
  262.3 3.5 copy-start.80
  262.3 3.5 copy-start.79
  262.3 3.5 copy-start.87
  262.3 3.6 copy-start.24
  266.8 3.4 copy-start.7
  270.1 3.7 copy-start.8
  273.9 4.9 %copy-start.1 = (f32[1774080]{0:T(1024)S(1)}, f32[1774080]{0:T(1024)}, u32[]{:S(2)}) copy-start(f32[1774080]{0:T(1024)} %constant_dynamic-update-slice_fusion) | copy-start | bytes 21288964
  289.1 160.8 %copy-start.33 = (f32[55440]{0:T(1024)S(1)}, f32[55440]{0:T(1024)}, u32[]{:S(2)}) copy-start(f32[55440]{0:T(1024)} %param.6) | copy-start | bytes 665284
  289.2 160.8 %copy-start.49 = (f32[55440]{0:T(1024)S(1)}, f32[55440]{0:T(1024)}, u32[]{:S(2)}) copy-start(f32[55440]{0:T(1024)} %param.7) | copy-start | bytes 665284
  289.2 160.8 %copy-start.50 = (f32[55440]{0:T(1024)S(1)}, f32[55440]{0:T(1024)}, u32[]{:S(2)}) copy-start(f32[55440]{0:T(1024)} %param.8) | copy-start | bytes 665284
  (47 other events, 78.8 us)
Sparse Core Ops, SparseCore 0:
  13.6 142.3 all-reduce.4
  284.4 165.5 all-reduce.6
where the time goes:
time: 460 us; the launch traced here: 459 us
  waiting for transfers between devices  296 us (64%)
  local copies, waits for them, and re-layouts  66.1 us (14%)
  matrix products  59.4 us (13%)
  other arithmetic  22.4 us (5%)
  between operations  14.9 us (3%)
    unnamed x4, waiting for transfers between devices  296 us
    unnamed x196, local copies, waits for them, and re-layouts  26.8 us
    dot_general x12, matrix products, product(): return jnp.einsum(spec, left, right, preferred_element_type=jnp.float32)  23.7 us
    dot_general x8, matrix products, token_sum(): lax.dot_general(left, right, (((0,), (0,)), ((), ())), preferred_element_...  15.9 us
  transfers between devices with their start and end apart: 2, of which 2 were waited for; matrix products, arithmetic and copies ran while one was open for 2% of the time, Pallas kernels for 0%

commit v1 on v0

--- a/solution.py
+++ b/solution.py
@@ -3,14 +3,265 @@
 import jax
 import jax.numpy as jnp
 from jax import lax
+from jax.experimental import pallas as pl
+from jax.experimental.pallas import tpu as pltpu
+import functools
 from jax.sharding import PartitionSpec as P
 
 D = 384
 HEADS = 6
 FF = 1536
 SEQ = 197
-MICRO = 2
 STEP = 3
+
+
+LANES = 128
+LINES = 4 * 1152 + 12
+
+
+def plan(devices, share):
+    bits = devices.bit_length() - 1
+    rows = -(-(share + D - 1) // D)
+    rows = -(-rows // 32) * 32
+    far = list(range(bits - 1, 2, -1))
+    orders = [far + [1, 2, 0], far + [2, 1, 0]]
+    half = rows // 2
+    if half % 16 == 0 and half > 16:
+        first = -(-half // 2 // 16) * 16
+        sizes = [first, first, half - first, half - first]
+    else:
+        sizes = [half, half]
+    parts = []
+    start = 0
+    for index, size in enumerate(sizes):
+        parts.append((start, size, orders[index % 2]))
+        start += size
+    return bits, rows, parts
+
+
+def place(device, order):
+    spot = 0
+    for index, bit in enumerate(order):
+        spot = spot + ((device // 2**bit) % 2) * 2**index
+    return spot
+
+
+def other(device, bit):
+    step = 2**bit
+    return device + step - 2 * step * ((device // step) % 2)
+
+
+def greet(me, bits):
+    barrier = pltpu.get_barrier_semaphore()
+    for bit in range(bits):
+        pl.semaphore_signal(
+            barrier, inc=1, device_id=(other(me, bit),), device_id_type=pl.DeviceIdType.MESH
+        )
+    pl.semaphore_wait(barrier, bits)
+
+
+def gather_kernel(devices, share, shard, w_qkv, w_out, w_up, w_down, tail, lines, *rest):
+    bits, rows, parts = plan(devices, share)
+    slots = rest[: len(parts)]
+    local_sem, send_sem, recv_sem = rest[len(parts) :]
+    me = lax.axis_index("dp")
+    own = []
+    for index, (start, size, order) in enumerate(parts):
+        copy = pltpu.make_async_copy(
+            shard.at[pl.ds(start, size)], slots[index].at[place(me, order)], local_sem.at[index]
+        )
+        copy.start()
+        own.append(copy)
+    greet(me, bits)
+    for copy in own:
+        copy.wait()
+    waiting = [None] * len(parts)
+    for stage in range(bits):
+        for index, (start, size, order) in enumerate(parts):
+            if waiting[index] is not None:
+                waiting[index].wait()
+            block = 2**stage
+            begin = (place(me, order) // block) * block
+            piece = slots[index].at[pl.ds(begin, block)]
+            copy = pltpu.make_async_remote_copy(
+                src_ref=piece,
+                dst_ref=piece,
+                send_sem=send_sem.at[index, stage],
+                recv_sem=recv_sem.at[index, stage],
+                device_id=(other(me, order[stage]),),
+                device_id_type=pl.DeviceIdType.MESH,
+            )
+            copy.start()
+            waiting[index] = copy
+    for copy in waiting:
+        copy.wait()
+    chunks = D // LANES
+    for device in range(devices):
+        first = device * share // D
+        shared = device * share % D != 0
+        for index, (start, size, order) in enumerate(parts):
+            spot = place(device, order)
+            at = first + start
+            for chunk in range(chunks):
+                if start == 0 and shared:
+                    before = lines[chunk, at : at + 1, :]
+                lines[chunk, at : at + size, :] = slots[index][
+                    spot, :, chunk * LANES : (chunk + 1) * LANES
+                ].astype(jnp.float32)
+                if start == 0 and shared:
+                    lines[chunk, at : at + 1, :] = lines[chunk, at : at + 1, :] + before
+    spread(lines, 0, w_qkv, 3)
+    spread(lines, 1152, w_out, 1)
+    spread(lines, 1536, w_up, 4)
+    spread(lines, 3072, w_down, 1)
+    spread(lines, 4608, tail, 1)
+
+
+def spread(lines, first, out, times):
+    height = out.shape[0]
+    for column in range(times):
+        for chunk in range(D // LANES):
+            if times == 1:
+                value = lines[chunk, first : first + height, :]
+            else:
+                value = lines[chunk, pl.ds(first + column, height, stride=times), :]
+            at = column * D + chunk * LANES
+            out[:, at : at + LANES] = value.astype(out.dtype)
+
+
+def gather_weights(params, devices):
+    share = params.shape[0]
+    bits, rows, parts = plan(devices, share)
+    offset = (lax.axis_index("dp") * share) % D
+    flat = jnp.zeros((rows * D,), jnp.float32)
+    flat = lax.dynamic_update_slice(flat, params, (offset,))
+    shard = flat.reshape(rows, D).astype(jnp.bfloat16)
+    vmem = pl.BlockSpec(memory_space=pltpu.VMEM)
+    return pl.pallas_call(
+        functools.partial(gather_kernel, devices, share),
+        out_shape=(
+            jax.ShapeDtypeStruct((D, 3 * D), jnp.bfloat16),
+            jax.ShapeDtypeStruct((D, D), jnp.bfloat16),
+            jax.ShapeDtypeStruct((D, FF), jnp.bfloat16),
+            jax.ShapeDtypeStruct((FF, D), jnp.bfloat16),
+            jax.ShapeDtypeStruct((16, D), jnp.float32),
+        ),
+        in_specs=[vmem],
+        out_specs=[vmem] * 5,
+        scratch_shapes=[pltpu.VMEM((D // LANES, LINES + rows + 24, LANES), jnp.float32)]
+        + [pltpu.VMEM((devices, size, D), jnp.bfloat16) for _, size, _ in parts]
+        + [
+            pltpu.SemaphoreType.DMA((len(parts),)),
+            pltpu.SemaphoreType.DMA((len(parts), bits)),
+            pltpu.SemaphoreType.DMA((len(parts), bits)),
+        ],
+        compiler_params=pltpu.CompilerParams(
+            collective_id=0, has_side_effects=True, vmem_limit_bytes=60 * 2**20
+        ),
+    )(shard)
+
+
+def scatter_kernel(devices, share, g_qkv, g_out, g_up, g_down, g_tail, out, lines, *rest):
+    bits, rows, parts = plan(devices, share)
+    count = len(parts)
+    slots, landed, sums = rest[:count], rest[count : 2 * count], rest[2 * count : 3 * count]
+    send_sem, recv_sem = rest[3 * count :]
+    me = lax.axis_index("dp")
+    collect(lines, 0, g_qkv, 3)
+    collect(lines, 1152, g_out, 1)
+    collect(lines, 1536, g_up, 4)
+    collect(lines, 3072, g_down, 1)
+    collect(lines, 4608, g_tail, 1)
+    lines[:, 4624:, :] = jnp.zeros_like(lines[:, 4624:, :])
+    for device in range(devices):
+        first = device * share // D
+        for index, (start, size, order) in enumerate(parts):
+            spot = place(device, order)
+            at = first + start
+            for chunk in range(D // LANES):
+                slots[index][spot, :, chunk * LANES : (chunk + 1) * LANES] = lines[
+                    chunk, at : at + size, :
+                ].astype(jnp.bfloat16)
+    greet(me, bits)
+    waiting = [None] * count
+
+    def send(index, stage):
+        order = parts[index][2]
+        block = 2**stage
+        spot = place(me, order) // block
+        away = spot + 1 - 2 * (spot % 2)
+        copy = pltpu.make_async_remote_copy(
+            src_ref=slots[index].at[pl.ds(away * block, block)],
+            dst_ref=landed[index].at[pl.ds(block - 1, block)],
+            send_sem=send_sem.at[index, stage],
+            recv_sem=recv_sem.at[index, stage],
+            device_id=(other(me, order[stage]),),
+            device_id_type=pl.DeviceIdType.MESH,
+        )
+        copy.start()
+        return copy
+
+    for index in range(count):
+        waiting[index] = send(index, bits - 1)
+    for stage in range(bits - 1, -1, -1):
+        for index, (start, size, order) in enumerate(parts):
+            waiting[index].wait()
+            block = 2**stage
+            begin = (place(me, order) // block) * block
+            if stage == 0:
+                piece = sums[index][begin] if bits > 1 else slots[index][begin].astype(jnp.float32)
+                out[start : start + size, :] = piece + landed[index][0].astype(jnp.float32)
+                continue
+
+            def add(step, carry, index=index, begin=begin, block=block, stage=stage):
+                spot = begin + step
+                if stage == bits - 1:
+                    old = slots[index][spot].astype(jnp.float32)
+                else:
+                    old = sums[index][spot]
+                new = old + landed[index][block - 1 + step].astype(jnp.float32)
+                sums[index][spot] = new
+                slots[index][spot] = new.astype(jnp.bfloat16)
+                return carry
+
+            lax.fori_loop(0, block, add, 0)
+            waiting[index] = send(index, stage - 1)
+
+
+def collect(lines, first, grads, times):
+    height = grads.shape[0]
+    for column in range(times):
+        for chunk in range(D // LANES):
+            at = column * D + chunk * LANES
+            value = grads[:, at : at + LANES]
+            if times == 1:
+                lines[chunk, first : first + height, :] = value
+            else:
+                lines[chunk, pl.ds(first + column, height, stride=times), :] = value
+
+
+def scatter_grads(grads, devices, share):
+    bits, rows, parts = plan(devices, share)
+    vmem = pl.BlockSpec(memory_space=pltpu.VMEM)
+    total = pl.pallas_call(
+        functools.partial(scatter_kernel, devices, share),
+        out_shape=jax.ShapeDtypeStruct((rows, D), jnp.float32),
+        in_specs=[vmem] * 5,
+        out_specs=vmem,
+        scratch_shapes=[pltpu.VMEM((D // LANES, LINES + rows + 24, LANES), jnp.float32)]
+        + [pltpu.VMEM((devices, size, D), jnp.bfloat16) for _, size, _ in parts]
+        + [pltpu.VMEM((devices, size, D), jnp.bfloat16) for _, size, _ in parts]
+        + [pltpu.VMEM((devices, size, D), jnp.float32) for _, size, _ in parts]
+        + [
+            pltpu.SemaphoreType.DMA((len(parts), bits)),
+            pltpu.SemaphoreType.DMA((len(parts), bits)),
+        ],
+        compiler_params=pltpu.CompilerParams(
+            collective_id=1, has_side_effects=True, vmem_limit_bytes=63 * 2**20
+        ),
+    )(*grads)
+    offset = (lax.axis_index("dp") * share) % D
+    return lax.dynamic_slice(total.reshape(-1), (offset,), (share,))
 
 
 def product(spec, left, right):
@@ -40,22 +291,6 @@
         grad_hat
         - jnp.mean(grad_hat, axis=-1, keepdims=True)
         - normed * jnp.mean(grad_hat * normed, axis=-1, keepdims=True)
-    )
-
-
-def unpack(flat):
-    first = 3 * D * D
-    second = first + D * D
-    third = second + D * FF
-    fourth = third + FF * D
-    fifth = fourth + 8 * D
-    return (
-        flat[:first].reshape(D, 3 * D),
-        flat[first:second].reshape(D, D),
-        flat[second:third].reshape(D, FF),
-        flat[third:fourth].reshape(FF, D),
-        flat[fourth:fifth].astype(jnp.float32).reshape(8, D),
-        flat[fifth:].astype(jnp.float32),
     )
 
 
@@ -172,17 +407,10 @@
             jnp.sum(grad_flat, axis=0),
         ]
     )
-    flat = jnp.concatenate(
-        [
-            grad_wqkv.reshape(-1),
-            grad_wout.reshape(-1),
-            grad_up.reshape(-1),
-            grad_down.reshape(-1),
-            vector_grads.reshape(-1),
-            jnp.sum(grad_pre, axis=0),
-        ]
-    )
-    return (grad_tokens, flat)
+    tail = jnp.concatenate(
+        [vector_grads, jnp.sum(grad_pre, axis=0).reshape(4, D), jnp.zeros((4, D), jnp.float32)]
+    )
+    return (grad_tokens, (grad_wqkv, grad_wout, grad_up, grad_down, tail))
 
 
 def adamw(params, grads, first, second, position):
@@ -209,30 +437,18 @@
 
 
 def per_device(tokens, params, moment1, moment2, cotangent):
-    shard_half = params.astype(jnp.bfloat16)
-    blocks = tokens.reshape(MICRO, -1, SEQ, D)
-    grad_blocks = cotangent.reshape(MICRO, -1, SEQ, D)
-    results = []
-    grads_in = []
-    running = None
-    shares = None
-    for micro in range(MICRO):
-        fwd_weights = unpack(lax.all_gather(shard_half, "dp", axis=0, tiled=True))
-        result, saved = forward(blocks[micro], fwd_weights)
-        bwd_weights = unpack(lax.all_gather(shard_half, "dp", axis=0, tiled=True))
-        grad_in, flat = backward(saved, grad_blocks[micro], bwd_weights)
-        results.append(result)
-        grads_in.append(grad_in)
-        running = flat if running is None else running + flat
-    shares = lax.psum_scatter(running, "dp", scatter_dimension=0, tiled=True)
-    count = tokens.shape[0] * tokens.shape[1] * lax.axis_size("dp")
+    devices = lax.axis_size("dp")
+    length = params.shape[0]
+    w_qkv, w_out, w_up, w_down, tail = gather_weights(params, devices)
+    weights = (w_qkv, w_out, w_up, w_down, tail[:8], tail[8:12].reshape(FF))
+    result, saved = forward(tokens, weights)
+    grad_tokens, grads = backward(saved, cotangent, weights)
+    shares = scatter_grads(grads, devices, length)
+    count = tokens.shape[0] * tokens.shape[1] * devices
     grad_params = shares * (1.0 / math.sqrt(count))
-    length = params.shape[0]
     position = lax.axis_index("dp") * length + jnp.arange(length, dtype=jnp.int32)
     new_params, new_first, new_second = adamw(params, grad_params, moment1, moment2, position)
-    result_all = jnp.concatenate(results, axis=0)
-    grad_all = jnp.concatenate(grads_in, axis=0)
-    return (result_all, grad_all, grad_params, new_params, new_first, new_second)
+    return (result, grad_tokens, grad_params, new_params, new_first, new_second)
 
 
 def solution(mesh):

time: 460 us -> 191 us (0.42)
  waiting for transfers between devices: 296 us -> 0 us
  Pallas kernels: 0 us -> 75.6 us
  local copies, waits for them, and re-layouts: 66.1 us -> 48.8 us
  between operations: 14.9 us -> 1.12 us
  matrix products: 59.4 us -> 49.2 us
  other arithmetic: 22.4 us -> 14.9 us
    unnamed x4 -> x0, waiting for transfers between devices: 296 us -> none
    pallas_call x0 -> x2, Pallas kernels: none -> 75.6 us  [the longest x1 38.1 us: gather_weights(): pl.pallas_call(functools.partial(gather_kernel, devices, share), out_shap...]
    unnamed x196 -> x54, local copies, waits for them, and re-layouts: 26.8 us -> 5.12 us
    slice x9 -> x1, local copies, waits for them, and re-layouts: 11.6 us -> 0.73 us  [per_device(): weights = (w_qkv, w_out, w_up, w_down, tail[:8], tail[8:12].reshape(FF))]
    reshape x10 -> x22, local copies, waits for them, and re-layouts: 19 us -> 28.5 us  [the longest x2 3.83 us: forward(): (projected[:, 2 * width:] + vectors[3]).astype(jnp.bfloat16)]
    dot_general x12 -> x6, matrix products: 23.7 us -> 15 us  [product(): return jnp.einsum(spec, left, right, preferred_element_type=jnp.float32)]
    dot_general x8 -> x4, matrix products: 15.9 us -> 9.23 us  [token_sum(): lax.dot_general(left, right, (((0,), (0,)), ((), ())), preferred_element_...]
    add x1, other arithmetic: 5.45 us -> 0.08 us  [forward(): hidden_mid + (jnp.dot(activated, w_down, preferred_element_type=jnp.float...]
  transfers between devices with their start and end apart: 2 -> 0, of which waited for: 2 -> 0; matrix products, arithmetic and copies ran while one was open for 2% -> 0% of each run, Pallas kernels for 0% -> 0%
where the time goes in v1:
time: 191 us; the launch traced here: 190 us
  Pallas kernels  75.6 us (40%)
  matrix products  49.2 us (26%)
  local copies, waits for them, and re-layouts  48.8 us (26%)
  other arithmetic  14.9 us (8%)
    pallas_call x1, Pallas kernels, gather_weights(): pl.pallas_call(functools.partial(gather_kernel, devices, share), out_shap...  38.1 us
    pallas_call x1, Pallas kernels, scatter_grads(): pl.pallas_call(functools.partial(scatter_kernel, devices, share), out_sha...  37.4 us
    dot_general x6, matrix products, product(): return jnp.einsum(spec, left, right, preferred_element_type=jnp.float32)  15 us
    dot_general x4, matrix products, times_t(): lax.dot_general(left, right, (((1,), (1,)), ((), ())), preferred_element_...  12 us
    dot_general x4, matrix products, token_sum(): lax.dot_general(left, right, (((0,), (0,)), ((), ())), preferred_element_...  9.23 us
    dot_general x1, matrix products, forward(): jnp.dot(mlp_input, w_up, preferred_element_type=jnp.float32) + up_bias  8.21 us
    unnamed x54, local copies, waits for them, and re-layouts  5.12 us
    reshape x2, local copies, waits for them, and re-layouts, forward(): (projected[:, 2 * width:] + vectors[3]).astype(jnp.bfloat16)  3.83 us

profile of v1, /device:TPU:0, one launch (start us, length us, event | category | flops | bytes accessed | tf_op | source)
XLA Modules:
  0.0 189.6 jit_solution(644382326372273379)
XLA Ops:
  0.7 2.4 %dynamic_update_slice.3 = bf16[61440]{0:T(1024)(128)(2,1)S(1)} dynamic-update-slice(bf16[61440]{0:T(1024)(128)(2,1)S(1)} %broadcast_in_dim.17, f32[55440]{0:T(1024)} %param.6, s32[]{:T(128)S(6)} %select_n.28) | dynamic-update-slice | bytes 443524 | tf_op jit(solution)/shard_map/dynamic_update_slice | solution.py:137
  3.8 38.1 %shard_map.100 = (bf16[384,1152]{1,0:T(8,128)(2,1)}, bf16[384,384]{1,0:T(8,128)(2,1)}, bf16[384,1536]{1,0:T(8,128)(2,1)}, bf16[1536,384]{1,0:T(8,128)(2,1)}, f32[16,384]{1,0:T(8,128)}) custom-call(bf16[160,384]{1,0:T(8,128)(2,1)} %convert_element_type.57.shard), custom_call_target="tpu_custom_call" | custom-call | tf_op jit(solution)/shard_map/pallas_call | solution.py:140
  42.0 1.0 slice_reduce_fusion
  43.0 1.4 reduce_sum.171
  44.5 1.3 multiply_reduce_fusion.7
  47.6 1.6 fusion.70
  50.2 1.5 reshape.167
  51.7 1.2 copy.128
  53.7 1.5 reshape.168
  55.7 1.7 multiply_reduce_fusion.1
  57.9 2.3 %reshape.166 = bf16[2,197,6,64]{3,2,1,0:T(8,128)(2,1)} reshape(bf16[394,384]{1,0:T(8,128)(2,1)} %get-tuple-element.67) | data formatting | bytes 605184 | tf_op jit(solution)/shard_map/reshape | solution.py:306
  60.2 1.5 copy.130
  62.4 1.1 copy.132
  63.6 1.2 reshape.152
  64.8 2.4 %convolution_add_fusion.2 = f32[394,384]{1,0:T(8,128)} fusion(bf16[394,384]{0,1:T(8,128)(2,1)S(1)} %reshape.152, bf16[384,384]{1,0:T(8,128)(2,1)} %get-tuple-element.13, f32[384]{0:T(512)S(1)} %get-tuple-element.47), kind=kOutput, calls=%fused_computation.41 | convolution fusion | flops 116346624 | bytes 1204224 | tf_op jit(solution)/shard_map/dot_general | solution.py:315
  67.3 2.0 %reshape.153 = f32[2,197,384]{2,1,0:T(8,128)} reshape(f32[394,384]{1,0:T(8,128)} %convolution_add_fusion.2) | data formatting | bytes 1210368 | tf_op jit(solution)/shard_map/reshape | solution.py:316
  69.2 1.2 fusion.63
  71.4 1.1 add_convert_fusion
  74.3 8.2 %fusion.4 = (bf16[394,1536]{1,0:T(8,128)(2,1)}, f32[394,1536]{1,0:T(8,128)}) fusion(f32[1536]{0:T(1024)S(1)} %add.162, bf16[394,384]{1,0:T(8,128)(2,1)S(1)} %reshape.154, bf16[384,1536]{1,0:T(8,128)(2,1)} %get-tuple-element.14), kind=kOutput, calls=%fused_computation.8 | convolution fusion | flops 504723456 | bytes 5119488 | tf_op jit(solution)/shard_map/dot_general | solution.py:319
  83.7 4.6 %fusion.69 = (f32[1536]{0:T(1024)S(1)}, bf16[394,1536]{1,0:T(8,128)(2,1)}) fusion(f32[394,1536]{1,0:T(8,128)} %get-tuple-element.83, bf16[1536,384]{1,0:T(8,128)(2,1)} %get-tuple-element.15, bf16[394,384]{1,0:T(8,128)(2,1)} %convert_element_type.67), kind=kOutput, calls=%fused_computation.119 | convolution fusion | flops 471436800 | bytes 5119488 | tf_op jit(solution)/shard_map/dot_general | solution.py:278
  88.3 2.0 %reshape.163 = f32[394,384]{1,0:T(8,128)} reshape(f32[2,197,384]{2,1,0:T(8,128)} %get-tuple-element.63) | data formatting | bytes 1210368 | tf_op jit(solution)/shard_map/reshape | solution.py:372
  90.2 3.4 %fusion.58 = (f32[384]{0:T(512)S(1)}, f32[384]{0:T(512)S(1)}, f32[394]{0:T(512)S(1)}, f32[394,384]{1,0:T(8,128)}) fusion(f32[394,384]{1,0:T(8,128)} %reshape.163, f32[384]{0:T(512)S(1)} %get-tuple-element.46, bf16[384,1536]{1,0:T(8,128)(2,1)} %get-tuple-element.14, bf16[394,1536]{1,0:T(8,128)(2,1)} %get-tuple-element.87), kind=kOutput, calls=%fused_computation.110 | convolution fusion | flops 465536640 | bytes 3606568 | tf_op jit(solution)/shard_map/dot_general | solution.py:278
  93.7 2.0 %reshape.156 = f32[2,197,384]{2,1,0:T(8,128)} reshape(f32[394,384]{1,0:T(8,128)} %get-tuple-element.73) | data formatting | bytes 1210368 | tf_op jit(solution)/shard_map/reshape | solution.py:374
  95.6 1.4 multiply_reduce_fusion.5
  97.1 1.7 fusion.60
  101.5 2.2 %convolution_convert_fusion.1 = bf16[394,384]{1,0:T(8,128)(2,1)} fusion(bf16[394,384]{1,0:T(8,128)(2,1)S(1)} %convert_element_type.70, bf16[384,384]{1,0:T(8,128)(2,1)} %get-tuple-element.13), kind=kOutput, calls=%fused_computation.47 | convolution fusion | flops 116346624 | bytes 900096 | tf_op jit(solution)/shard_map/dot_general | solution.py:278
  103.7 2.3 %reshape.169 = bf16[2,197,6,64]{3,2,1,0:T(8,128)(2,1)} reshape(bf16[394,384]{1,0:T(8,128)(2,1)} %convolution_convert_fusion.1) | data formatting | bytes 605184 | tf_op jit(solution)/shard_map/reshape | solution.py:379
  106.0 1.5 copy.137
  108.2 1.2 copy.147
  109.3 2.0 %reshape.160 = bf16[394,384]{0,1:T(8,128)(2,1)} reshape(bf16[2,197,6,64]{1,0,3,2:T(2,128)(2,1)} %copy.147) | data formatting | bytes 605184 | tf_op jit(solution)/shard_map/reshape | solution.py:390
  111.3 3.0 %fusion.71 = f32[2,6,197,197]{2,3,1,0:T(8,128)} fusion(bf16[2,197,6,64]{1,3,2,0:T(8,128)(2,1)S(1)} %copy.137, bf16[2,197,6,64]{1,3,2,0:T(8,128)(2,1)} %copy-done.19), kind=kOutput, calls=%fused_computation.121 | convolution fusion | flops 59610624 | bytes 2468016 | tf_op jit(solution)/shard_map/bqhe,bkhe->bhqk/dot_general | solution.py:268
  114.3 4.5 %fusion.36 = bf16[2,197,6,64]{1,3,2,0:T(8,128)(2,1)} fusion(bf16[2,197,6,64]{1,3,2,0:T(8,128)(2,1)} %copy.128, f32[2,6,197,197]{2,3,1,0:T(8,128)} %fusion.71, f32[2,6,197,197]{2,3,1,0:T(8,128)S(1)} %get-tuple-element.81, f32[2,6,197]{2,1,0:T(8,128)S(1)} %log_add_fusion), kind=kOutput, calls=%fused_computation.49 | convolution fusion | flops 63955852 | bytes 4340304 | tf_op jit(solution)/shard_map/bhqk,bqhe->bkhe/dot_general | solution.py:268
  118.8 2.1 %copy.144 = bf16[2,197,6,64]{1,0,3,2:T(2,128)(2,1)} copy(bf16[2,197,6,64]{1,3,2,0:T(8,128)(2,1)} %fusion.36) | data formatting | bytes 605184 | tf_op jit(solution)/shard_map/bhqk,bqhe->bkhe/transpose | solution.py:268
  121.0 2.0 %reshape.159 = bf16[394,384]{0,1:T(8,128)(2,1)} reshape(bf16[2,197,6,64]{1,0,3,2:T(2,128)(2,1)} %copy.144) | data formatting | bytes 605184 | tf_op jit(solution)/shard_map/reshape | solution.py:389
  123.0 4.4 %fusion.65 = (f32[6,64]{1,0:T(8,128)S(1)}, bf16[2,197,6,64]{1,3,2,0:T(8,128)(2,1)}) fusion(bf16[2,197,6,64]{1,3,2,0:T(8,128)(2,1)S(1)} %copy-done.18, f32[2,6,197,197]{2,3,1,0:T(8,128)} %fusion.71, f32[2,6,197]{2,1,0:T(8,128)S(1)} %log_add_fusion, f32[2,6,197,197]{2,3,1,0:T(8,128)S(1)} %get-tuple-element.81), kind=kOutput, calls=%fused_computation.117 | convolution fusion | flops 64106764 | bytes 4341840 | tf_op jit(solution)/shard_map/bhqk,bkhe->bqhe/dot_general | solution.py:268
  127.4 1.5 copy.141
  131.0 1.1 reshape.162
  132.2 1.7 fusion.59
  134.1 1.2 concatenate.8.g_tail
  135.4 3.6 %fusion.41.g_up = f32[384,1536]{1,0:T(8,128)} fusion(bf16[394,384]{1,0:T(8,128)(2,1)} %copy-done.16, bf16[394,1536]{1,0:T(8,128)(2,1)} %get-tuple-element.87), kind=kOutput, calls=%fused_computation.61 | convolution fusion | flops 464781312 | bytes 3872256 | tf_op jit(solution)/shard_map/dot_general | solution.py:272
  139.0 1.2 fusion.73.g_out
  140.2 2.0 %fusion.72.g_qkv = f32[384,1152]{1,0:T(8,128)} fusion(bf16[394,384]{1,0:T(8,128)(2,1)S(1)} %copy-done.13, bf16[394,1152]{0,1:T(8,128)(2,1)S(1)} %constant_dynamic-update-slice_fusion), kind=kOutput, calls=%fused_computation.122 | convolution fusion | flops 348585984 | bytes 2979840 | tf_op jit(solution)/shard_map/dot_general | solution.py:272
  142.2 2.4 %fusion.74.g_down = f32[1536,384]{1,0:T(8,128)} fusion(bf16[394,1536]{1,0:T(8,128)(2,1)S(1)} %copy-done.5, bf16[394,384]{1,0:T(8,128)(2,1)S(1)} %copy-done.22), kind=kOutput, calls=%fused_computation.124 | convolution fusion | flops 464781312 | bytes 3872256 | tf_op jit(solution)/shard_map/dot_general | solution.py:272
  144.6 37.4 %shard_map.101 = f32[160,384]{1,0:T(8,128)} custom-call(f32[384,1152]{1,0:T(8,128)} %fusion.72.g_qkv, f32[384,384]{1,0:T(8,128)} %fusion.73.g_out, f32[384,1536]{1,0:T(8,128)} %fusion.41.g_up, f32[1536,384]{1,0:T(8,128)} %fusion.74.g_down, f32[16,384]{1,0:T(8,128)} %concatenate.8.g_tail), custom_call_target="tpu_custom_call" | custom-call | tf_op jit(solution)/shard_map/pallas_call | solution.py:246
  182.1 1.1 reshape.165
  183.1 2.3 %multiply_subtract_fusion = (f32[55440]{0:T(1024)}, f32[55440]{0:T(1024)}, f32[55440]{0:T(1024)}, f32[55440]{0:T(1024)}) fusion(f32[55440]{0:T(1024)S(1)} %copy-done.23, s32[]{:T(128)S(6)} %mul.193, f32[61440]{0:T(1024)S(1)} %reshape.165, s32[]{:T(128)S(6)} %select_n.28, f32[55440]{0:T(1024)} %param.7, f32[55440]{0:T(1024)} %param.8), kind=kLoop, calls=%fused_computation.75 | loop fusion | flops 1386000 | bytes 1774088 | tf_op jit(solution)/shard_map/sub | solution.py:436
  186.2 1.1 copy.149
  188.5 1.1 copy.148
  (101 shorter events, 17.4 us)
Async XLA Ops:
  0.6 45.2 %copy-start = (f32[2,197,384]{2,0,1:T(2,128)S(1)}, f32[2,197,384]{2,0,1:T(2,128)}, u32[]{:S(2)}) copy-start(f32[2,197,384]{2,0,1:T(2,128)} %param.5) | copy-start | bytes 1815556
  42.0 5.7 %copy-start.7 = (bf16[384,1152]{1,0:T(8,128)(2,1)S(1)}, bf16[384,1152]{1,0:T(8,128)(2,1)}, u32[]{:S(2)}) copy-start(bf16[384,1152]{1,0:T(8,128)(2,1)} %get-tuple-element.12) | copy-start | bytes 2654212
  55.7 2.2 %copy-start.17 = (bf16[2,197,6,64]{1,3,2,0:T(8,128)(2,1)}, bf16[2,197,6,64]{1,3,2,0:T(8,128)(2,1)S(1)}, u32[]{:S(2)}) copy-start(bf16[2,197,6,64]{1,3,2,0:T(8,128)(2,1)S(1)} %copy.129) | copy-start | bytes 907780
  61.7 0.8 copy-start.19
  64.8 5.9 %copy-start.9 = (bf16[394,384]{0,1:T(8,128)(2,1)}, bf16[394,384]{0,1:T(8,128)(2,1)S(1)}, u32[]{:S(2)}) copy-start(bf16[394,384]{0,1:T(8,128)(2,1)S(1)} %reshape.152) | copy-start | bytes 907780
  70.5 0.9 copy-start.1
  73.5 9.0 %copy-start.16 = (bf16[394,384]{1,0:T(8,128)(2,1)}, bf16[394,384]{1,0:T(8,128)(2,1)S(1)}, u32[]{:S(2)}) copy-start(bf16[394,384]{1,0:T(8,128)(2,1)S(1)} %reshape.154) | copy-start | bytes 907780
  74.2 8.2 %copy-start.15 = (f32[2,197,384]{2,0,1:T(2,128)S(1)}, f32[2,197,384]{2,0,1:T(2,128)}, u32[]{:S(2)}) copy-start(f32[2,197,384]{2,0,1:T(2,128)} %param.9) | copy-start | bytes 1815556
  98.8 0.9 copy-start.3
  101.5 2.2 %copy-start.11 = (bf16[394,384]{1,0:T(8,128)(2,1)}, bf16[394,384]{1,0:T(8,128)(2,1)S(1)}, u32[]{:S(2)}) copy-start(bf16[394,384]{1,0:T(8,128)(2,1)S(1)} %convert_element_type.70) | copy-start | bytes 907780
  114.3 8.7 %copy-start.18 = (bf16[2,197,6,64]{1,3,2,0:T(8,128)(2,1)S(1)}, bf16[2,197,6,64]{1,3,2,0:T(8,128)(2,1)}, u32[]{:S(2)}) copy-start(bf16[2,197,6,64]{1,3,2,0:T(8,128)(2,1)} %copy-done.17) | copy-start | bytes 907780
  127.4 3.6 %copy-start.21 = (bf16[394,384]{0,1:T(8,128)(2,1)S(1)}, bf16[394,384]{0,1:T(8,128)(2,1)}, u32[]{:S(2)}) copy-start(bf16[394,384]{0,1:T(8,128)(2,1)} %reshape.159) | copy-start | bytes 907780
  127.4 3.6 %copy-start.20 = (bf16[394,384]{0,1:T(8,128)(2,1)S(1)}, bf16[394,384]{0,1:T(8,128)(2,1)}, u32[]{:S(2)}) copy-start(bf16[394,384]{0,1:T(8,128)(2,1)} %reshape.160) | copy-start | bytes 907780
  127.4 4.8 %copy-start.8 = (bf16[384,1152]{1,0:T(8,128)(2,1)S(1)}, bf16[384,1152]{1,0:T(8,128)(2,1)}, u32[]{:S(2)}) copy-start(bf16[384,1152]{1,0:T(8,128)(2,1)} %get-tuple-element.12) | copy-start | bytes 2654212
  133.9 5.1 %copy-start.10 = (bf16[394,384]{0,1:T(8,128)(2,1)S(1)}, bf16[394,384]{0,1:T(8,128)(2,1)}, u32[]{:S(2)}) copy-start(bf16[394,384]{0,1:T(8,128)(2,1)} %copy-done.9) | copy-start | bytes 907780
  133.9 5.1 %copy-start.12 = (bf16[394,384]{1,0:T(8,128)(2,1)S(1)}, bf16[394,384]{1,0:T(8,128)(2,1)}, u32[]{:S(2)}) copy-start(bf16[394,384]{1,0:T(8,128)(2,1)} %copy-done.11) | copy-start | bytes 907780
  135.4 4.8 %copy-start.13 = (bf16[394,384]{1,0:T(8,128)(2,1)S(1)}, bf16[394,384]{1,0:T(8,128)(2,1)}, u32[]{:S(2)}) copy-start(bf16[394,384]{1,0:T(8,128)(2,1)} %reshape.148) | copy-start | bytes 907780
  139.0 3.2 %copy-start.5 = (bf16[394,1536]{1,0:T(8,128)(2,1)S(1)}, bf16[394,1536]{1,0:T(8,128)(2,1)}, u32[]{:S(2)}) copy-start(bf16[394,1536]{1,0:T(8,128)(2,1)} %get-tuple-element.82) | copy-start | bytes 3631108
  139.0 3.2 %copy-start.22 = (bf16[394,384]{1,0:T(8,128)(2,1)S(1)}, bf16[394,384]{1,0:T(8,128)(2,1)}, u32[]{:S(2)}) copy-start(bf16[394,384]{1,0:T(8,128)(2,1)} %convert_element_type.67) | copy-start | bytes 907780
  144.6 38.5 %copy-start.23 = (f32[55440]{0:T(1024)S(1)}, f32[55440]{0:T(1024)}, u32[]{:S(2)}) copy-start(f32[55440]{0:T(1024)} %param.6) | copy-start | bytes 665284
  182.0 3.3 %copy-start.14 = (f32[394,384]{1,0:T(8,128)S(1)}, f32[394,384]{1,0:T(8,128)}, u32[]{:S(2)}) copy-start(f32[394,384]{1,0:T(8,128)} %get-tuple-element.75) | copy-start | bytes 1815556
  182.1 3.8 %copy-start.4 = (f32[2,197,384]{2,1,0:T(8,128)S(1)}, f32[2,197,384]{2,1,0:T(8,128)}, u32[]{:S(2)}) copy-start(f32[2,197,384]{2,1,0:T(8,128)} %copy-done.3) | copy-start | bytes 1815556
  185.5 1.9 copy-start.6
  185.9 1.4 copy-start.24
  187.3 1.1 copy-start.2

commit v2 on v1

--- a/solution.py
+++ b/solution.py
@@ -264,10 +264,6 @@
     return lax.dynamic_slice(total.reshape(-1), (offset,), (share,))
 
 
-def product(spec, left, right):
-    return jnp.einsum(spec, left, right, preferred_element_type=jnp.float32)
-
-
 def token_sum(left, right):
     return lax.dot_general(
         left, right, (((0,), (0,)), ((), ())), preferred_element_type=jnp.float32
@@ -294,123 +290,219 @@
     )
 
 
-def forward(tokens_mb, weights):
-    w_qkv, w_out, w_up, w_down, vectors, up_bias = weights
-    batch, length, width = tokens_mb.shape
-    normed_in, scale_in = layer_norm(tokens_mb)
-    attn_input = (normed_in * vectors[0] + vectors[1]).astype(jnp.bfloat16).reshape(-1, width)
-    projected = jnp.dot(attn_input, w_qkv, preferred_element_type=jnp.float32)
-    heads_shape = (batch, length, HEADS, width // HEADS)
-    query_half = (projected[:, :width] + vectors[2]).astype(jnp.bfloat16).reshape(heads_shape)
-    key_half = projected[:, width : 2 * width].astype(jnp.bfloat16).reshape(heads_shape)
-    value_half = (projected[:, 2 * width :] + vectors[3]).astype(jnp.bfloat16).reshape(heads_shape)
-    scores = product("bqhe,bkhe->bhqk", query_half, key_half) * (width // HEADS) ** (-0.5)
-    top = jnp.max(scores, axis=-1, keepdims=True)
-    raw_weights = jnp.exp(scores - top)
-    total = jnp.sum(raw_weights, axis=-1, keepdims=True)
-    log_total = top + jnp.log(total)
-    probs = (raw_weights / total).astype(jnp.bfloat16)
-    context = product("bhqk,bkhe->bqhe", probs, value_half).astype(jnp.bfloat16).reshape(-1, width)
-    hidden_mid = tokens_mb + (
-        jnp.dot(context, w_out, preferred_element_type=jnp.float32) + vectors[4]
-    ).reshape(tokens_mb.shape)
-    normed_mid, scale_mid = layer_norm(hidden_mid)
-    mlp_input = (normed_mid * vectors[5] + vectors[6]).astype(jnp.bfloat16).reshape(-1, width)
-    pre_act = jnp.dot(mlp_input, w_up, preferred_element_type=jnp.float32) + up_bias
-    activated = jax.nn.gelu(pre_act, approximate=False).astype(jnp.bfloat16)
-    result = hidden_mid + (
-        jnp.dot(activated, w_down, preferred_element_type=jnp.float32) + vectors[7]
-    ).reshape(tokens_mb.shape)
-    saved = (
-        normed_in,
-        scale_in,
-        attn_input,
-        query_half,
-        key_half,
-        value_half,
-        log_total,
-        context,
-        normed_mid,
-        scale_mid,
-        mlp_input,
-        pre_act,
-        activated,
-    )
-    return (result, saved)
-
-
-def backward(saved, grad_result, weights):
-    w_qkv, w_out, w_up, w_down, vectors, up_bias = weights
-    (
-        normed_in,
-        scale_in,
-        attn_input,
-        query_half,
-        key_half,
-        value_half,
-        log_total,
-        context,
-        normed_mid,
-        scale_mid,
-        mlp_input,
-        pre_act,
-        activated,
-    ) = saved
-    width = grad_result.shape[-1]
-    grad_flat = grad_result.reshape(-1, width)
-    grad_half = grad_flat.astype(jnp.bfloat16)
-    grad_down = token_sum(activated, grad_half)
-    grad_act = times_t(grad_half, w_down)
-    slope = (
-        0.5 * (1.0 + jax.scipy.special.erf(pre_act * 0.7071067811865476))
-        + pre_act * jnp.exp(-0.5 * pre_act * pre_act) * 0.3989422804014327
-    )
-    grad_pre = grad_act * slope
-    grad_pre_half = grad_pre.astype(jnp.bfloat16)
-    grad_up = token_sum(mlp_input, grad_pre_half)
-    grad_mlp_in = times_t(grad_pre_half, w_up)
-    mid_flat = normed_mid.reshape(-1, width)
-    grad_hidden = grad_result + norm_back(
-        (grad_mlp_in * vectors[5]).reshape(grad_result.shape), normed_mid, scale_mid
-    )
-    hidden_flat = grad_hidden.reshape(-1, width)
-    hidden_half = hidden_flat.astype(jnp.bfloat16)
-    grad_wout = token_sum(context, hidden_half)
-    grad_context = times_t(hidden_half, w_out).astype(jnp.bfloat16).reshape(query_half.shape)
-    scale_factor = (width // HEADS) ** (-0.5)
-    scores = product("bqhe,bkhe->bhqk", query_half, key_half) * scale_factor
-    probs_full = jnp.exp(scores - log_total)
-    probs_half = probs_full.astype(jnp.bfloat16)
-    grad_value = product("bhqk,bqhe->bkhe", probs_half, grad_context)
-    grad_probs = product("bqhe,bkhe->bhqk", grad_context, value_half)
-    delta = jnp.sum(probs_full * grad_probs, axis=-1, keepdims=True)
-    grad_scores = (probs_full * (grad_probs - delta) * scale_factor).astype(jnp.bfloat16)
-    grad_query = product("bhqk,bkhe->bqhe", grad_scores, key_half).reshape(-1, width)
-    grad_key = product("bhqk,bqhe->bkhe", grad_scores, query_half).reshape(-1, width)
-    grad_value = grad_value.reshape(-1, width)
-    proj_half = jnp.concatenate([grad_query, grad_key, grad_value], axis=1).astype(jnp.bfloat16)
-    grad_wqkv = token_sum(attn_input, proj_half)
-    grad_attn_in = times_t(proj_half, w_qkv)
-    in_flat = normed_in.reshape(-1, width)
-    grad_tokens = grad_hidden + norm_back(
-        (grad_attn_in * vectors[0]).reshape(grad_result.shape), normed_in, scale_in
-    )
-    vector_grads = jnp.stack(
-        [
-            jnp.sum(grad_attn_in * in_flat, axis=0),
-            jnp.sum(grad_attn_in, axis=0),
-            jnp.sum(grad_query, axis=0),
-            jnp.sum(grad_value, axis=0),
-            jnp.sum(hidden_flat, axis=0),
-            jnp.sum(grad_mlp_in * mid_flat, axis=0),
-            jnp.sum(grad_mlp_in, axis=0),
-            jnp.sum(grad_flat, axis=0),
-        ]
-    )
-    tail = jnp.concatenate(
-        [vector_grads, jnp.sum(grad_pre, axis=0).reshape(4, D), jnp.zeros((4, D), jnp.float32)]
-    )
-    return (grad_tokens, (grad_wqkv, grad_wout, grad_up, grad_down, tail))
+PAD = -(-SEQ // 16) * 16
+DEEP = D // HEADS
+
+
+def dot(left, right):
+    return lax.dot_general(
+        left, right, (((1,), (0,)), ((), ())), preferred_element_type=jnp.float32
+    )
+
+
+def column_sum(values):
+    return jnp.sum(values, axis=0, keepdims=True)
+
+
+def block_kernel(
+    images,
+    tokens,
+    cotangent,
+    w_qkv,
+    w_out,
+    w_up,
+    w_down,
+    tail,
+    result,
+    grad_tokens,
+    g_qkv,
+    g_out,
+    g_up,
+    g_down,
+    g_tail,
+    x,
+    dy,
+    xhat,
+    mid,
+    a16,
+    c16,
+    q16,
+    k16,
+    v16,
+    o16,
+    probs,
+    wide,
+    slope,
+    act16,
+    du16,
+    dh,
+    do16,
+    dqkv,
+    dqkv16,
+):
+    rows = images * PAD
+    bf16 = jnp.bfloat16
+    for image in range(images):
+        for here, there in ((x, tokens), (dy, cotangent)):
+            begin = image * PAD
+            last = SEQ // 8 * 8
+            here[begin + last : begin + PAD, :] = jnp.zeros((PAD - last, D), jnp.float32)
+            here[begin : begin + SEQ, :] = there[image]
+    normed, factor_in = layer_norm(x[...])
+    xhat[...] = normed
+    a16[...] = (normed * tail[0:1, :] + tail[1:2, :]).astype(bf16)
+    q16[...] = (dot(a16[...], w_qkv[:, 0:D]) + tail[2:3, :]).astype(bf16)
+    k16[...] = dot(a16[...], w_qkv[:, D : 2 * D]).astype(bf16)
+    v16[...] = (dot(a16[...], w_qkv[:, 2 * D :]) + tail[3:4, :]).astype(bf16)
+    scale = DEEP ** (-0.5)
+    inside = lax.broadcasted_iota(jnp.int32, (PAD, PAD), 1) < SEQ
+
+    def attend(image, carry):
+        span = pl.ds(pl.multiple_of(image * PAD, 16), PAD)
+        for head in range(HEADS):
+            at = slice(head * DEEP, (head + 1) * DEEP)
+            scores = times_t(q16[span, at], k16[span, at]) * scale
+            scores = jnp.where(inside, scores, -1e30)
+            raw = jnp.exp(scores - jnp.max(scores, axis=-1, keepdims=True))
+            full = raw / jnp.sum(raw, axis=-1, keepdims=True)
+            probs[image, head] = full
+            o16[span, at] = dot(full.astype(bf16), v16[span, at]).astype(bf16)
+        return carry
+
+    lax.fori_loop(0, images, attend, 0)
+    hidden = x[...] + (dot(o16[...], w_out[...]) + tail[4:5, :])
+    x[...] = hidden
+    normed, factor_mid = layer_norm(hidden)
+    mid[...] = normed
+    c16[...] = (normed * tail[5:6, :] + tail[6:7, :]).astype(bf16)
+    for column in range(FF // D):
+        at = slice(column * D, (column + 1) * D)
+        wide[:, at] = dot(c16[...], w_up[:, at]) + tail[8 + column : 9 + column, :]
+    step = 16
+
+    def gelu(index, carry):
+        span = pl.ds(pl.multiple_of(index * step, step), step)
+        pre = wide[span, :]
+        phi = 0.5 * (1.0 + lax.erf(pre * 0.7071067811865476))
+        act16[span, :] = (pre * phi).astype(bf16)
+        slope[span, :] = phi + pre * jnp.exp(-0.5 * pre * pre) * 0.3989422804014327
+        return carry
+
+    lax.fori_loop(0, rows // step, gelu, 0)
+    final = x[...] + (dot(act16[...], w_down[...]) + tail[7:8, :])
+    for image in range(images):
+        result[image] = final[image * PAD : image * PAD + SEQ, :]
+
+    dy16 = dy[...].astype(bf16)
+    g_down[...] = token_sum(act16[...], dy16)
+    g_tail[7:8, :] = column_sum(dy[...])
+    wide[...] = times_t(dy16, w_down[...])
+
+    def grad_pre(index, total):
+        span = pl.ds(pl.multiple_of(index * step, step), step)
+        value = wide[span, :] * slope[span, :]
+        du16[span, :] = value.astype(bf16)
+        return total + value
+
+    total = lax.fori_loop(0, rows // step, grad_pre, jnp.zeros((step, FF), jnp.float32))
+    total = column_sum(total)
+    for column in range(FF // D):
+        g_tail[8 + column : 9 + column, :] = total[:, column * D : (column + 1) * D]
+    g_tail[12:16, :] = jnp.zeros((4, D), jnp.float32)
+    g_up[...] = token_sum(c16[...], du16[...])
+    grad_mlp = times_t(du16[...], w_up[...])
+    g_tail[5:6, :] = column_sum(grad_mlp * mid[...])
+    g_tail[6:7, :] = column_sum(grad_mlp)
+    grad_hidden = dy[...] + norm_back(grad_mlp * tail[5:6, :], mid[...], factor_mid)
+    dh[...] = grad_hidden
+    g_tail[4:5, :] = column_sum(grad_hidden)
+    dh16 = grad_hidden.astype(bf16)
+    g_out[...] = token_sum(o16[...], dh16)
+    do16[...] = times_t(dh16, w_out[...]).astype(bf16)
+
+    def attend_back(image, carry):
+        span = pl.ds(pl.multiple_of(image * PAD, 16), PAD)
+        for head in range(HEADS):
+            at = slice(head * DEEP, (head + 1) * DEEP)
+            full = probs[image, head]
+            grad_o = do16[span, at]
+            dqkv[span, 2 * D + head * DEEP : 2 * D + (head + 1) * DEEP] = token_sum(
+                full.astype(bf16), grad_o
+            )
+            grad_probs = times_t(grad_o, v16[span, at])
+            delta = jnp.sum(full * grad_probs, axis=-1, keepdims=True)
+            grad_scores = (full * (grad_probs - delta) * scale).astype(bf16)
+            dqkv[span, at] = dot(grad_scores, k16[span, at])
+            dqkv[span, D + head * DEEP : D + (head + 1) * DEEP] = token_sum(
+                grad_scores, q16[span, at]
+            )
+        return carry
+
+    lax.fori_loop(0, images, attend_back, 0)
+    g_tail[2:3, :] = column_sum(dqkv[:, 0:D])
+    g_tail[3:4, :] = column_sum(dqkv[:, 2 * D :])
+    dqkv16[...] = dqkv[...].astype(bf16)
+    g_qkv[...] = token_sum(a16[...], dqkv16[...])
+    grad_in = times_t(dqkv16[...], w_qkv[...])
+    g_tail[0:1, :] = column_sum(grad_in * xhat[...])
+    g_tail[1:2, :] = column_sum(grad_in)
+    final = dh[...] + norm_back(grad_in * tail[0:1, :], xhat[...], factor_in)
+    for image in range(images):
+        grad_tokens[image] = final[image * PAD : image * PAD + SEQ, :]
+
+
+def block_scratch(images):
+    rows = images * PAD
+    f32, bf16 = jnp.float32, jnp.bfloat16
+    return [
+        pltpu.VMEM(shape, kind)
+        for shape, kind in (
+            ((rows, D), f32),
+            ((rows, D), f32),
+            ((rows, D), f32),
+            ((rows, D), f32),
+            ((rows, D), bf16),
+            ((rows, D), bf16),
+            ((rows, D), bf16),
+            ((rows, D), bf16),
+            ((rows, D), bf16),
+            ((rows, D), bf16),
+            ((images, HEADS, PAD, PAD), f32),
+            ((rows, FF), f32),
+            ((rows, FF), f32),
+            ((rows, FF), bf16),
+            ((rows, FF), bf16),
+            ((rows, D), f32),
+            ((rows, D), bf16),
+            ((rows, 3 * D), f32),
+            ((rows, 3 * D), bf16),
+        )
+    ]
+
+
+def block(tokens, cotangent, weights):
+    images = tokens.shape[0]
+    f32 = jnp.float32
+    vmem = pl.BlockSpec(memory_space=pltpu.VMEM)
+    return pl.pallas_call(
+        functools.partial(block_kernel, images),
+        out_shape=tuple(
+            jax.ShapeDtypeStruct(shape, f32)
+            for shape in (
+                tokens.shape,
+                tokens.shape,
+                (D, 3 * D),
+                (D, D),
+                (D, FF),
+                (FF, D),
+                (16, D),
+            )
+        ),
+        in_specs=[vmem] * 7,
+        out_specs=[vmem] * 7,
+        scratch_shapes=block_scratch(images),
+        compiler_params=pltpu.CompilerParams(vmem_limit_bytes=63 * 2**20),
+    )(tokens, cotangent, *weights)
 
 
 def adamw(params, grads, first, second, position):
@@ -439,10 +531,8 @@
 def per_device(tokens, params, moment1, moment2, cotangent):
     devices = lax.axis_size("dp")
     length = params.shape[0]
-    w_qkv, w_out, w_up, w_down, tail = gather_weights(params, devices)
-    weights = (w_qkv, w_out, w_up, w_down, tail[:8], tail[8:12].reshape(FF))
-    result, saved = forward(tokens, weights)
-    grad_tokens, grads = backward(saved, cotangent, weights)
+    weights = gather_weights(params, devices)
+    result, grad_tokens, *grads = block(tokens, cotangent, weights)
     shares = scatter_grads(grads, devices, length)
     count = tokens.shape[0] * tokens.shape[1] * devices
     grad_params = shares * (1.0 / math.sqrt(count))

time: 191 us -> 111 us (0.58)
  matrix products: 49.2 us -> 0 us
  local copies, waits for them, and re-layouts: 48.8 us -> 10.3 us
  Pallas kernels: 75.6 us -> 97.9 us
  other arithmetic: 14.9 us -> 1.2 us
    dot_general x18 -> x0, matrix products: 49.2 us -> none  [the longest x6 15 us: product(): return jnp.einsum(spec, left, right, preferred_element_type=jnp.float32)]
    reshape x21 -> x0, local copies, waits for them, and re-layouts: 27.5 us -> none  [the longest x2 3.83 us: forward(): (projected[:, 2 * width:] + vectors[3]).astype(jnp.bfloat16)]
    pallas_call x0 -> x1, Pallas kernels: none -> 22.4 us  [block(): pl.pallas_call(functools.partial(block_kernel, images), out_shape=tuple((...]
    reduce_sum x9 -> x0, other arithmetic: 8.4 us -> none  [the longest x2 2.59 us: layer_norm(): center = values - jnp.mean(values, axis=-1, keepdims=True)]
    convert_element_type x4 -> x0, local copies, waits for them, and re-layouts: 3.01 us -> none  [the longest x1 1.15 us: forward(): product('bhqk,bkhe->bqhe', probs, value_half).astype(jnp.bfloat16)]
    another operation x10 -> x0, local copies, waits for them, and re-layouts: 2.85 us -> none
    convert_element_type x3 -> x0, other arithmetic: 2.77 us -> none  [the longest x1 1.11 us: forward(): (normed_mid * vectors[5] + vectors[6]).astype(jnp.bfloat16)]
    slice x3 -> x0, local copies, waits for them, and re-layouts: 2.55 us -> none  [the longest x1 1.04 us: forward(): vectors[7]]
where the time goes in v2:
time: 111 us; the launch traced here: 110 us
  Pallas kernels  97.9 us (88%)
  local copies, waits for them, and re-layouts  10.3 us (9%)
  other arithmetic  1.2 us (1%)
    pallas_call x1, Pallas kernels, gather_weights(): pl.pallas_call(functools.partial(gather_kernel, devices, share), out_shap...  38.1 us
    pallas_call x1, Pallas kernels, scatter_grads(): pl.pallas_call(functools.partial(scatter_kernel, devices, share), out_sha...  37.3 us
    pallas_call x1, Pallas kernels, block(): pl.pallas_call(functools.partial(block_kernel, images), out_shape=tuple((...  22.4 us
    unnamed x14, local copies, waits for them, and re-layouts  6.19 us
    dynamic_update_slice x1, local copies, waits for them, and re-layouts, gather_weights(): flat = lax.dynamic_update_slice(flat, params, (offset,))  2.39 us

profile of v2, /device:TPU:0, one launch (start us, length us, event | category | flops | bytes accessed | tf_op | source)
XLA Modules:
  0.0 110.2 jit_solution(11653972214064991721)
XLA Ops:
  0.6 0.0 copy-start.2
  0.7 2.4 %dynamic_update_slice.3 = bf16[61440]{0:T(1024)(128)(2,1)S(1)} dynamic-update-slice(bf16[61440]{0:T(1024)(128)(2,1)S(1)} %broadcast_in_dim.17, f32[55440]{0:T(1024)} %param.6, s32[]{:T(128)S(6)} %select_n.28) | dynamic-update-slice | bytes 443524 | tf_op jit(solution)/shard_map/dynamic_update_slice | solution.py:137
  3.1 0.7 convert_element_type.6.shard
  3.8 2.0 %copy.11.tokens = f32[2,197,384]{2,1,0:T(8,128)} copy(f32[2,197,384]{2,0,1:T(2,128)} %param.5) | data formatting | bytes 1210368 | tf_op args[0]
  5.8 0.0 copy-done.2
  5.8 0.9 copy.12.cotangent
  6.6 38.1 %shard_map.100 = (bf16[384,1152]{1,0:T(8,128)(2,1)}, bf16[384,384]{1,0:T(8,128)(2,1)}, bf16[384,1536]{1,0:T(8,128)(2,1)}, bf16[1536,384]{1,0:T(8,128)(2,1)}, f32[16,384]{1,0:T(8,128)}) custom-call(bf16[160,384]{1,0:T(8,128)(2,1)} %convert_element_type.6.shard), custom_call_target="tpu_custom_call" | custom-call | tf_op jit(solution)/shard_map/pallas_call | solution.py:140
  44.8 22.4 %shard_map.101 = (f32[2,197,384]{2,1,0:T(8,128)}, f32[2,197,384]{2,1,0:T(8,128)}, f32[384,1152]{1,0:T(8,128)}, f32[384,384]{1,0:T(8,128)}, f32[384,1536]{1,0:T(8...) custom-call(f32[2,197,384]{2,1,0:T(8,128)} %copy.11.tokens, f32[2,197,384]{2,1,0:T(8,128)} %copy.12.cotangent, ...), custom_call_target="tpu_custom_call" | custom-call | tf_op jit(solution)/shard_map/pallas_call | solution.py:487
  67.2 2.2 %copy.13 = f32[2,197,384]{2,0,1:T(2,128)} copy(f32[2,197,384]{2,1,0:T(8,128)} %get-tuple-element.30) | data formatting | bytes 1210368
  69.4 0.0 copy-start.1
  69.4 37.3 %shard_map.102 = f32[160,384]{1,0:T(8,128)} custom-call(f32[384,1152]{1,0:T(8,128)} %get-tuple-element.25.g_qkv, f32[384,384]{1,0:T(8,128)} %get-tuple-element.26.g_out, f32[384,1536]{1,0:T(8,128)} %get-tuple-element.27.g_up, f32[1536,384]{1,0:T(8,128)} %get-tuple-element.28.g_down, f32[16,384]{1,0:T(8,128)} %get-tuple-element.29.g_tail), custom_call_target="tpu_custom_call" | custom-call | tf_op jit(solution)/shard_map/pallas_call | solution.py:246
  106.8 0.0 copy-start
  106.8 0.0 copy-start.3
  106.8 0.0 copy-start.4
  106.8 1.0 reshape.17
  107.8 0.0 copy-done.1
  107.8 1.1 %copy.14 = f32[2,197,384]{2,0,1:T(2,128)} copy(f32[2,197,384]{2,1,0:T(8,128)S(1)} %copy-done.1) | data formatting | bytes 1210368
  109.0 0.0 copy-done
  109.0 0.0 copy-done.3
  109.0 0.0 copy-done.4
  109.0 1.2 %multiply_subtract_fusion = (f32[55440]{0:T(1024)}, f32[55440]{0:T(1024)}, f32[55440]{0:T(1024)}, f32[55440]{0:T(1024)}) fusion(f32[55440]{0:T(1024)S(1)} %copy-done, s32[]{:T(128)S(6)} %mul.43, f32[61440]{0:T(1024)S(1)} %reshape.17, s32[]{:T(128)S(6)} %select_n.28, f32[55440]{0:T(1024)S(1)} %copy-done.3, f32[55440]{0:T(1024)S(1)} %copy-done.4), kind=kLoop, calls=%fused_computation | loop fusion | flops 1386000 | bytes 1774088 | tf_op jit(solution)/shard_map/sub | solution.py:528
  (1 shorter events, 0.0 us)
Async XLA Ops:
  0.6 5.1 %copy-start.2 = (f32[2,197,384]{2,0,1:T(2,128)S(1)}, f32[2,197,384]{2,0,1:T(2,128)}, u32[]{:S(2)}) copy-start(f32[2,197,384]{2,0,1:T(2,128)} %param.9) | copy-start | bytes 1815556
  69.4 38.4 %copy-start.1 = (f32[2,197,384]{2,1,0:T(8,128)S(1)}, f32[2,197,384]{2,1,0:T(8,128)}, u32[]{:S(2)}) copy-start(f32[2,197,384]{2,1,0:T(8,128)} %get-tuple-element.31) | copy-start | bytes 1815556
  106.8 2.2 %copy-start = (f32[55440]{0:T(1024)S(1)}, f32[55440]{0:T(1024)}, u32[]{:S(2)}) copy-start(f32[55440]{0:T(1024)} %param.6) | copy-start | bytes 665284
  106.8 2.2 %copy-start.3 = (f32[55440]{0:T(1024)S(1)}, f32[55440]{0:T(1024)}, u32[]{:S(2)}) copy-start(f32[55440]{0:T(1024)} %param.7) | copy-start | bytes 665284
  106.8 2.2 %copy-start.4 = (f32[55440]{0:T(1024)S(1)}, f32[55440]{0:T(1024)}, u32[]{:S(2)}) copy-start(f32[55440]{0:T(1024)} %param.8) | copy-start | bytes 665284

commit v3 on v2

--- a/solution.py
+++ b/solution.py
@@ -19,23 +19,22 @@
 LINES = 4 * 1152 + 12
 
 
-def plan(devices, share):
+def plan(devices, share, late=False):
     bits = devices.bit_length() - 1
     rows = -(-(share + D - 1) // D)
     rows = -(-rows // 32) * 32
     far = list(range(bits - 1, 2, -1))
     orders = [far + [1, 2, 0], far + [2, 1, 0]]
-    half = rows // 2
-    if half % 16 == 0 and half > 16:
-        first = -(-half // 2 // 16) * 16
-        sizes = [first, first, half - first, half - first]
-    else:
-        sizes = [half, half]
+    units = rows // 32
+    waves = min(3, units)
+    sizes = [16 * (units * (wave + 1) // waves - units * wave // waves) for wave in range(waves)]
+    sizes.sort(reverse=late)
     parts = []
     start = 0
-    for index, size in enumerate(sizes):
-        parts.append((start, size, orders[index % 2]))
-        start += size
+    for size in sizes:
+        for order in orders:
+            parts.append((start, size, order))
+            start += size
     return bits, rows, parts
 
 
@@ -76,8 +75,12 @@
     for copy in own:
         copy.wait()
     waiting = [None] * len(parts)
-    for stage in range(bits):
+    pairs = len(parts) // 2
+    for wave in range(bits + pairs - 1):
         for index, (start, size, order) in enumerate(parts):
+            stage = wave - index // 2
+            if not 0 <= stage < bits:
+                continue
             if waiting[index] is not None:
                 waiting[index].wait()
             block = 2**stage
@@ -162,7 +165,7 @@
 
 
 def scatter_kernel(devices, share, g_qkv, g_out, g_up, g_down, g_tail, out, lines, *rest):
-    bits, rows, parts = plan(devices, share)
+    bits, rows, parts = plan(devices, share, True)
     count = len(parts)
     slots, landed, sums = rest[:count], rest[count : 2 * count], rest[2 * count : 3 * count]
     send_sem, recv_sem = rest[3 * count :]
@@ -173,15 +176,17 @@
     collect(lines, 3072, g_down, 1)
     collect(lines, 4608, g_tail, 1)
     lines[:, 4624:, :] = jnp.zeros_like(lines[:, 4624:, :])
-    for device in range(devices):
-        first = device * share // D
-        for index, (start, size, order) in enumerate(parts):
+
+    def pack(index):
+        start, size, order = parts[index]
+        for device in range(devices):
             spot = place(device, order)
-            at = first + start
+            at = device * share // D + start
             for chunk in range(D // LANES):
                 slots[index][spot, :, chunk * LANES : (chunk + 1) * LANES] = lines[
                     chunk, at : at + size, :
                 ].astype(jnp.bfloat16)
+
     greet(me, bits)
     waiting = [None] * count
 
@@ -201,10 +206,15 @@
         copy.start()
         return copy
 
-    for index in range(count):
-        waiting[index] = send(index, bits - 1)
-    for stage in range(bits - 1, -1, -1):
+    for wave in range(bits + count // 2):
         for index, (start, size, order) in enumerate(parts):
+            stage = bits - wave + index // 2
+            if not 0 <= stage <= bits:
+                continue
+            if stage == bits:
+                pack(index)
+                waiting[index] = send(index, bits - 1)
+                continue
             waiting[index].wait()
             block = 2**stage
             begin = (place(me, order) // block) * block
@@ -241,7 +251,7 @@
 
 
 def scatter_grads(grads, devices, share):
-    bits, rows, parts = plan(devices, share)
+    bits, rows, parts = plan(devices, share, True)
     vmem = pl.BlockSpec(memory_space=pltpu.VMEM)
     total = pl.pallas_call(
         functools.partial(scatter_kernel, devices, share),

time: 111 us -> 114 us (1.027)
  Pallas kernels: 97.9 us -> 101 us
    pallas_call x1, Pallas kernels: 38.1 us -> 40.3 us  [gather_weights(): pl.pallas_call(functools.partial(gather_kernel, devices, share), out_shap...]
    pallas_call x1, Pallas kernels: 37.3 us -> 38.6 us  [scatter_grads(): pl.pallas_call(functools.partial(scatter_kernel, devices, share), out_sha...]
where the time goes in v3:
time: 114 us
  Pallas kernels  101 us (89%)
  local copies, waits for them, and re-layouts  10.3 us (9%)
  other arithmetic  1.2 us (1%)
    pallas_call x1, Pallas kernels, gather_weights(): pl.pallas_call(functools.partial(gather_kernel, devices, share), out_shap...  40.3 us
    pallas_call x1, Pallas kernels, scatter_grads(): pl.pallas_call(functools.partial(scatter_kernel, devices, share), out_sha...  38.6 us
    pallas_call x1, Pallas kernels, block(): pl.pallas_call(functools.partial(block_kernel, images), out_shape=tuple((...  22.5 us
    unnamed x14, local copies, waits for them, and re-layouts  6.19 us
    dynamic_update_slice x1, local copies, waits for them, and re-layouts, gather_weights(): flat = lax.dynamic_update_slice(flat, params, (offset,))  2.39 us

profile of v3, /device:TPU:0, one launch (start us, length us, event | category | flops | bytes accessed | tf_op | source)
XLA Modules:
  0.0 113.6 jit_solution(11850552985458696921)
XLA Ops:
  0.6 0.0 copy-start.2
  0.7 2.4 %dynamic_update_slice.3 = bf16[61440]{0:T(1024)(128)(2,1)S(1)} dynamic-update-slice(bf16[61440]{0:T(1024)(128)(2,1)S(1)} %broadcast_in_dim.17, f32[55440]{0:T(1024)} %param.6, s32[]{:T(128)S(6)} %select_n.28) | dynamic-update-slice | bytes 443524 | tf_op jit(solution)/shard_map/dynamic_update_slice | solution.py:140
  3.1 0.7 convert_element_type.6.shard
  3.8 2.0 %copy.11.tokens = f32[2,197,384]{2,1,0:T(8,128)} copy(f32[2,197,384]{2,0,1:T(2,128)} %param.5) | data formatting | bytes 1210368 | tf_op args[0]
  5.8 0.0 copy-done.2
  5.8 0.9 copy.12.cotangent
  6.6 40.3 %shard_map.100 = (bf16[384,1152]{1,0:T(8,128)(2,1)}, bf16[384,384]{1,0:T(8,128)(2,1)}, bf16[384,1536]{1,0:T(8,128)(2,1)}, bf16[1536,384]{1,0:T(8,128)(2,1)}, f32[16,384]{1,0:T(8,128)}) custom-call(bf16[160,384]{1,0:T(8,128)(2,1)} %convert_element_type.6.shard), custom_call_target="tpu_custom_call" | custom-call | tf_op jit(solution)/shard_map/pallas_call | solution.py:143
  46.9 22.5 %shard_map.101 = (f32[2,197,384]{2,1,0:T(8,128)}, f32[2,197,384]{2,1,0:T(8,128)}, f32[384,1152]{1,0:T(8,128)}, f32[384,384]{1,0:T(8,128)}, f32[384,1536]{1,0:T(8...) custom-call(f32[2,197,384]{2,1,0:T(8,128)} %copy.11.tokens, f32[2,197,384]{2,1,0:T(8,128)} %copy.12.cotangent, ...), custom_call_target="tpu_custom_call" | custom-call | tf_op jit(solution)/shard_map/pallas_call | solution.py:497
  69.4 2.2 %copy.13 = f32[2,197,384]{2,0,1:T(2,128)} copy(f32[2,197,384]{2,1,0:T(8,128)} %get-tuple-element.30) | data formatting | bytes 1210368
  71.6 0.0 copy-start.1
  71.6 38.6 %shard_map.102 = f32[160,384]{1,0:T(8,128)} custom-call(f32[384,1152]{1,0:T(8,128)} %get-tuple-element.25.g_qkv, f32[384,384]{1,0:T(8,128)} %get-tuple-element.26.g_out, f32[384,1536]{1,0:T(8,128)} %get-tuple-element.27.g_up, f32[1536,384]{1,0:T(8,128)} %get-tuple-element.28.g_down, f32[16,384]{1,0:T(8,128)} %get-tuple-element.29.g_tail), custom_call_target="tpu_custom_call" | custom-call | tf_op jit(solution)/shard_map/pallas_call | solution.py:256
  110.2 0.0 copy-start
  110.2 0.0 copy-start.3
  110.2 0.0 copy-start.4
  110.2 1.0 reshape.17
  111.3 0.0 copy-done.1
  111.3 1.1 copy.14
  112.4 0.0 copy-done
  112.4 0.0 copy-done.3
  112.4 0.0 copy-done.4
  112.4 1.2 %multiply_subtract_fusion = (f32[55440]{0:T(1024)}, f32[55440]{0:T(1024)}, f32[55440]{0:T(1024)}, f32[55440]{0:T(1024)}) fusion(f32[55440]{0:T(1024)S(1)} %copy-done, s32[]{:T(128)S(6)} %mul.43, f32[61440]{0:T(1024)S(1)} %reshape.17, s32[]{:T(128)S(6)} %select_n.28, f32[55440]{0:T(1024)S(1)} %copy-done.3, f32[55440]{0:T(1024)S(1)} %copy-done.4), kind=kLoop, calls=%fused_computation | loop fusion | flops 1386000 | bytes 1774088 | tf_op jit(solution)/shard_map/sub | solution.py:538
  (1 shorter events, 0.0 us)
Async XLA Ops:
  0.6 5.1 %copy-start.2 = (f32[2,197,384]{2,0,1:T(2,128)S(1)}, f32[2,197,384]{2,0,1:T(2,128)}, u32[]{:S(2)}) copy-start(f32[2,197,384]{2,0,1:T(2,128)} %param.9) | copy-start | bytes 1815556
  71.6 39.7 %copy-start.1 = (f32[2,197,384]{2,1,0:T(8,128)S(1)}, f32[2,197,384]{2,1,0:T(8,128)}, u32[]{:S(2)}) copy-start(f32[2,197,384]{2,1,0:T(8,128)} %get-tuple-element.31) | copy-start | bytes 1815556
  110.2 2.2 %copy-start = (f32[55440]{0:T(1024)S(1)}, f32[55440]{0:T(1024)}, u32[]{:S(2)}) copy-start(f32[55440]{0:T(1024)} %param.6) | copy-start | bytes 665284
  110.2 2.2 %copy-start.3 = (f32[55440]{0:T(1024)S(1)}, f32[55440]{0:T(1024)}, u32[]{:S(2)}) copy-start(f32[55440]{0:T(1024)} %param.7) | copy-start | bytes 665284
  110.2 2.2 %copy-start.4 = (f32[55440]{0:T(1024)S(1)}, f32[55440]{0:T(1024)}, u32[]{:S(2)}) copy-start(f32[55440]{0:T(1024)} %param.8) | copy-start | bytes 665284

commit v4 on v2

--- a/solution.py
+++ b/solution.py
@@ -173,15 +173,17 @@
     collect(lines, 3072, g_down, 1)
     collect(lines, 4608, g_tail, 1)
     lines[:, 4624:, :] = jnp.zeros_like(lines[:, 4624:, :])
-    for device in range(devices):
-        first = device * share // D
-        for index, (start, size, order) in enumerate(parts):
+
+    def pack(index):
+        start, size, order = parts[index]
+        for device in range(devices):
             spot = place(device, order)
-            at = first + start
+            at = device * share // D + start
             for chunk in range(D // LANES):
                 slots[index][spot, :, chunk * LANES : (chunk + 1) * LANES] = lines[
                     chunk, at : at + size, :
                 ].astype(jnp.bfloat16)
+
     greet(me, bits)
     waiting = [None] * count
 
@@ -202,6 +204,7 @@
         return copy
 
     for index in range(count):
+        pack(index)
         waiting[index] = send(index, bits - 1)
     for stage in range(bits - 1, -1, -1):
         for index, (start, size, order) in enumerate(parts):
@@ -347,7 +350,7 @@
             begin = image * PAD
             last = SEQ // 8 * 8
             here[begin + last : begin + PAD, :] = jnp.zeros((PAD - last, D), jnp.float32)
-            here[begin : begin + SEQ, :] = there[image]
+            here[begin : begin + SEQ, :] = there[:, image, :]
     normed, factor_in = layer_norm(x[...])
     xhat[...] = normed
     a16[...] = (normed * tail[0:1, :] + tail[1:2, :]).astype(bf16)
@@ -391,7 +394,7 @@
     lax.fori_loop(0, rows // step, gelu, 0)
     final = x[...] + (dot(act16[...], w_down[...]) + tail[7:8, :])
     for image in range(images):
-        result[image] = final[image * PAD : image * PAD + SEQ, :]
+        result[:, image, :] = final[image * PAD : image * PAD + SEQ, :]
 
     dy16 = dy[...].astype(bf16)
     g_down[...] = token_sum(act16[...], dy16)
@@ -448,7 +451,7 @@
     g_tail[1:2, :] = column_sum(grad_in)
     final = dh[...] + norm_back(grad_in * tail[0:1, :], xhat[...], factor_in)
     for image in range(images):
-        grad_tokens[image] = final[image * PAD : image * PAD + SEQ, :]
+        grad_tokens[:, image, :] = final[image * PAD : image * PAD + SEQ, :]
 
 
 def block_scratch(images):
@@ -481,7 +484,7 @@
 
 
 def block(tokens, cotangent, weights):
-    images = tokens.shape[0]
+    images = tokens.shape[1]
     f32 = jnp.float32
     vmem = pl.BlockSpec(memory_space=pltpu.VMEM)
     return pl.pallas_call(
@@ -532,7 +535,10 @@
     devices = lax.axis_size("dp")
     length = params.shape[0]
     weights = gather_weights(params, devices)
-    result, grad_tokens, *grads = block(tokens, cotangent, weights)
+    result, grad_tokens, *grads = block(
+        tokens.transpose(1, 0, 2), cotangent.transpose(1, 0, 2), weights
+    )
+    result, grad_tokens = result.transpose(1, 0, 2), grad_tokens.transpose(1, 0, 2)
     shares = scatter_grads(grads, devices, length)
     count = tokens.shape[0] * tokens.shape[1] * devices
     grad_params = shares * (1.0 / math.sqrt(count))

time: 111 us -> 104 us (0.937)
  local copies, waits for them, and re-layouts: 10.3 us -> 4.04 us
    unnamed x14 -> x6, local copies, waits for them, and re-layouts: 6.19 us -> 0.01 us
where the time goes in v4:
time: 104 us
  Pallas kernels  97.9 us (94%)
  local copies, waits for them, and re-layouts  4.04 us (4%)
  other arithmetic  1.21 us (1%)
    pallas_call x1, Pallas kernels, gather_weights(): pl.pallas_call(functools.partial(gather_kernel, devices, share), out_shap...  38.1 us
    pallas_call x1, Pallas kernels, scatter_grads(): pl.pallas_call(functools.partial(scatter_kernel, devices, share), out_sha...  36.9 us
    pallas_call x1, Pallas kernels, block(): pl.pallas_call(functools.partial(block_kernel, images), out_shape=tuple((...  22.8 us
    dynamic_update_slice x1, local copies, waits for them, and re-layouts, gather_weights(): flat = lax.dynamic_update_slice(flat, params, (offset,))  2.34 us

profile of v4, /device:TPU:0, one launch (start us, length us, event | category | flops | bytes accessed | tf_op | source)
XLA Modules:
  0.0 103.9 jit_solution(13258737236664260431)
XLA Ops:
  0.7 2.3 %dynamic_update_slice.3 = bf16[61440]{0:T(1024)(128)(2,1)S(1)} dynamic-update-slice(bf16[61440]{0:T(1024)(128)(2,1)S(1)} %broadcast_in_dim.17, f32[55440]{0:T(1024)} %param.6, s32[]{:T(128)S(6)} %select_n.28) | dynamic-update-slice | bytes 443524 | tf_op jit(solution)/shard_map/dynamic_update_slice | solution.py:137
  3.0 0.7 convert_element_type.6.shard
  3.7 38.1 %shard_map.100 = (bf16[384,1152]{1,0:T(8,128)(2,1)}, bf16[384,384]{1,0:T(8,128)(2,1)}, bf16[384,1536]{1,0:T(8,128)(2,1)}, bf16[1536,384]{1,0:T(8,128)(2,1)}, f32[16,384]{1,0:T(8,128)}) custom-call(bf16[160,384]{1,0:T(8,128)(2,1)} %convert_element_type.6.shard), custom_call_target="tpu_custom_call" | custom-call | tf_op jit(solution)/shard_map/pallas_call | solution.py:140
  41.9 22.8 %shard_map.101 = (f32[197,2,384]{2,1,0:T(2,128)}, f32[197,2,384]{2,1,0:T(2,128)}, f32[384,1152]{1,0:T(8,128)}, f32[384,384]{1,0:T(8,128)}, f32[384,1536]{1,0:T(8...) custom-call(f32[197,2,384]{2,1,0:T(2,128)} %bitcast.4, f32[197,2,384]{2,1,0:T(2,128)} %bitcast.5, ...), custom_call_target="tpu_custom_call" | custom-call | tf_op jit(solution)/shard_map/pallas_call | solution.py:490
  64.7 0.0 copy-start
  64.7 0.0 copy-start.1
  64.7 0.0 copy-start.2
  64.7 36.9 %shard_map.102 = f32[160,384]{1,0:T(8,128)} custom-call(f32[384,1152]{1,0:T(8,128)} %get-tuple-element.25.g_qkv, f32[384,384]{1,0:T(8,128)} %get-tuple-element.26.g_out, f32[384,1536]{1,0:T(8,128)} %get-tuple-element.27.g_up, f32[1536,384]{1,0:T(8,128)} %get-tuple-element.28.g_down, f32[16,384]{1,0:T(8,128)} %get-tuple-element.29.g_tail), custom_call_target="tpu_custom_call" | custom-call | tf_op jit(solution)/shard_map/pallas_call | solution.py:249
  101.7 1.0 reshape.17
  102.6 0.0 copy-done
  102.7 0.0 copy-done.1
  102.7 0.0 copy-done.2
  102.7 1.2 %multiply_subtract_fusion = (f32[55440]{0:T(1024)}, f32[55440]{0:T(1024)}, f32[55440]{0:T(1024)}, f32[55440]{0:T(1024)}) fusion(f32[55440]{0:T(1024)S(1)} %copy-done, s32[]{:T(128)S(6)} %mul.43, f32[61440]{0:T(1024)S(1)} %reshape.17, s32[]{:T(128)S(6)} %select_n.28, f32[55440]{0:T(1024)S(1)} %copy-done.1, f32[55440]{0:T(1024)S(1)} %copy-done.2), kind=kLoop, calls=%fused_computation | loop fusion | flops 1386000 | bytes 1774088 | tf_op jit(solution)/shard_map/sub | solution.py:531
  (1 shorter events, 0.0 us)
Async XLA Ops:
  64.7 37.9 %copy-start = (f32[55440]{0:T(1024)S(1)}, f32[55440]{0:T(1024)}, u32[]{:S(2)}) copy-start(f32[55440]{0:T(1024)} %param.6) | copy-start | bytes 665284
  64.7 37.9 %copy-start.1 = (f32[55440]{0:T(1024)S(1)}, f32[55440]{0:T(1024)}, u32[]{:S(2)}) copy-start(f32[55440]{0:T(1024)} %param.7) | copy-start | bytes 665284
  64.7 37.9 %copy-start.2 = (f32[55440]{0:T(1024)S(1)}, f32[55440]{0:T(1024)}, u32[]{:S(2)}) copy-start(f32[55440]{0:T(1024)} %param.8) | copy-start | bytes 665284

commit v5 on v4

--- a/solution.py
+++ b/solution.py
@@ -24,17 +24,16 @@
     rows = -(-(share + D - 1) // D)
     rows = -(-rows // 32) * 32
     far = list(range(bits - 1, 2, -1))
-    orders = [far + [1, 2, 0], far + [2, 1, 0]]
+    orders = [far + [1, 2, 0], far + [2, 1, 0], [1, 2] + far + [0], [2, 1] + far + [0]]
     half = rows // 2
     if half % 16 == 0 and half > 16:
-        first = -(-half // 2 // 16) * 16
-        sizes = [first, first, half - first, half - first]
+        sizes = [half - 16, half - 16, 16, 16]
     else:
         sizes = [half, half]
     parts = []
     start = 0
     for index, size in enumerate(sizes):
-        parts.append((start, size, orders[index % 2]))
+        parts.append((start, size, orders[index]))
         start += size
     return bits, rows, parts
 

time: 104 us -> 102 us (0.981)
  Pallas kernels: 97.9 us -> 95.5 us
    pallas_call x1, Pallas kernels: 36.9 us -> 35.2 us  [scatter_grads(): pl.pallas_call(functools.partial(scatter_kernel, devices, share), out_sha...]
where the time goes in v5:
time: 102 us
  Pallas kernels  95.5 us (94%)
  local copies, waits for them, and re-layouts  4.04 us (4%)
  other arithmetic  1.21 us (1%)
    pallas_call x1, Pallas kernels, gather_weights(): pl.pallas_call(functools.partial(gather_kernel, devices, share), out_shap...  37.5 us
    pallas_call x1, Pallas kernels, scatter_grads(): pl.pallas_call(functools.partial(scatter_kernel, devices, share), out_sha...  35.2 us
    pallas_call x1, Pallas kernels, block(): pl.pallas_call(functools.partial(block_kernel, images), out_shape=tuple((...  22.8 us
    dynamic_update_slice x1, local copies, waits for them, and re-layouts, gather_weights(): flat = lax.dynamic_update_slice(flat, params, (offset,))  2.34 us

profile of v5, /device:TPU:0, one launch (start us, length us, event | category | flops | bytes accessed | tf_op | source)
XLA Modules:
  0.0 101.5 jit_solution(14802163590543474852)
XLA Ops:
  0.7 2.3 %dynamic_update_slice.3 = bf16[61440]{0:T(1024)(128)(2,1)S(1)} dynamic-update-slice(bf16[61440]{0:T(1024)(128)(2,1)S(1)} %broadcast_in_dim.17, f32[55440]{0:T(1024)} %param.6, s32[]{:T(128)S(6)} %select_n.28) | dynamic-update-slice | bytes 443524 | tf_op jit(solution)/shard_map/dynamic_update_slice | solution.py:136
  3.0 0.7 convert_element_type.6.shard
  3.7 37.5 %shard_map.100 = (bf16[384,1152]{1,0:T(8,128)(2,1)}, bf16[384,384]{1,0:T(8,128)(2,1)}, bf16[384,1536]{1,0:T(8,128)(2,1)}, bf16[1536,384]{1,0:T(8,128)(2,1)}, f32[16,384]{1,0:T(8,128)}) custom-call(bf16[160,384]{1,0:T(8,128)(2,1)} %convert_element_type.6.shard), custom_call_target="tpu_custom_call" | custom-call | tf_op jit(solution)/shard_map/pallas_call | solution.py:139
  41.3 22.8 %shard_map.101 = (f32[197,2,384]{2,1,0:T(2,128)}, f32[197,2,384]{2,1,0:T(2,128)}, f32[384,1152]{1,0:T(8,128)}, f32[384,384]{1,0:T(8,128)}, f32[384,1536]{1,0:T(8...) custom-call(f32[197,2,384]{2,1,0:T(2,128)} %bitcast.4, f32[197,2,384]{2,1,0:T(2,128)} %bitcast.5, ...), custom_call_target="tpu_custom_call" | custom-call | tf_op jit(solution)/shard_map/pallas_call | solution.py:489
  64.1 0.0 copy-start
  64.1 0.0 copy-start.1
  64.1 0.0 copy-start.2
  64.1 35.2 %shard_map.102 = f32[160,384]{1,0:T(8,128)} custom-call(f32[384,1152]{1,0:T(8,128)} %get-tuple-element.25.g_qkv, f32[384,384]{1,0:T(8,128)} %get-tuple-element.26.g_out, f32[384,1536]{1,0:T(8,128)} %get-tuple-element.27.g_up, f32[1536,384]{1,0:T(8,128)} %get-tuple-element.28.g_down, f32[16,384]{1,0:T(8,128)} %get-tuple-element.29.g_tail), custom_call_target="tpu_custom_call" | custom-call | tf_op jit(solution)/shard_map/pallas_call | solution.py:248
  99.3 1.0 reshape.17
  100.3 0.0 copy-done
  100.3 0.0 copy-done.1
  100.3 0.0 copy-done.2
  100.3 1.2 %multiply_subtract_fusion = (f32[55440]{0:T(1024)}, f32[55440]{0:T(1024)}, f32[55440]{0:T(1024)}, f32[55440]{0:T(1024)}) fusion(f32[55440]{0:T(1024)S(1)} %copy-done, s32[]{:T(128)S(6)} %mul.43, f32[61440]{0:T(1024)S(1)} %reshape.17, s32[]{:T(128)S(6)} %select_n.28, f32[55440]{0:T(1024)S(1)} %copy-done.1, f32[55440]{0:T(1024)S(1)} %copy-done.2), kind=kLoop, calls=%fused_computation | loop fusion | flops 1386000 | bytes 1774088 | tf_op jit(solution)/shard_map/sub | solution.py:530
  (1 shorter events, 0.0 us)
Async XLA Ops:
  64.1 36.2 %copy-start = (f32[55440]{0:T(1024)S(1)}, f32[55440]{0:T(1024)}, u32[]{:S(2)}) copy-start(f32[55440]{0:T(1024)} %param.6) | copy-start | bytes 665284
  64.1 36.2 %copy-start.1 = (f32[55440]{0:T(1024)S(1)}, f32[55440]{0:T(1024)}, u32[]{:S(2)}) copy-start(f32[55440]{0:T(1024)} %param.7) | copy-start | bytes 665284
  64.1 36.2 %copy-start.2 = (f32[55440]{0:T(1024)S(1)}, f32[55440]{0:T(1024)}, u32[]{:S(2)}) copy-start(f32[55440]{0:T(1024)} %param.8) | copy-start | bytes 665284
